TPU v7x, 32 devices: a whole 2x2x4 slice. The times are simulated.
32 devices in a mesh: dp: 8 (over z, y), tensor: 4 (over x, core).
Axes of the slice: x: 2, y: 2, z: 4, core: 2. Of those that a mesh axis runs over, the one named last changes fastest.
Arguments:
- tokens: bfloat16 [16384, 1024], P(('dp', 'tensor')), may hold values from -6 to 6
- cotangent: bfloat16 [16384, 1024], P(('dp', 'tensor')), may hold values from -6 to 6
- segment_ids: int32 [16384], P('dp'), may hold values from 0 to 1023, as said below
- positions: int32 [16384], P('dp'), may hold values from 0 to 1023, as said below
- attention_entry: float32 [1024, 3, 1024], P('dp', None, 'tensor'), may hold values from -0.1875 to 0.1875
- attention_exit: float32 [1024, 1024], P('tensor', 'dp'), may hold values from -0.375 to 0.375
- feedforward_entry: float32 [1024, 2, 2624], P('dp', None, 'tensor'), may hold values from -0.1875 to 0.1875
- feedforward_exit: float32 [2624, 1024], P('tensor', 'dp'), may hold values from -0.125 to 0.125
- norm_gains: float32 [2, 1024], P(None, 'dp'), may hold values from 0.5 to 1.5
- momentum_attention_entry: float32 [1024, 3, 1024], P('dp', None, 'tensor'), may hold values from -40 to 40
- momentum_attention_exit: float32 [1024, 1024], P('tensor', 'dp'), may hold values from -40 to 40
- momentum_feedforward_entry: float32 [1024, 2, 2624], P('dp', None, 'tensor'), may hold values from -40 to 40
- momentum_feedforward_exit: float32 [2624, 1024], P('tensor', 'dp'), may hold values from -40 to 40
- momentum_norm_gains: float32 [2, 1024], P(None, 'dp'), may hold values from -40 to 40
- variance_attention_entry: float32 [1024, 3, 1024], P('dp', None, 'tensor'), may hold values from 32.768 to 819.2
- variance_attention_exit: float32 [1024, 1024], P('tensor', 'dp'), may hold values from 32.768 to 819.2
- variance_feedforward_entry: float32 [1024, 2, 2624], P('dp', None, 'tensor'), may hold values from 32.768 to 819.2
- variance_feedforward_exit: float32 [2624, 1024], P('tensor', 'dp'), may hold values from 32.768 to 819.2
- variance_norm_gains: float32 [2, 1024], P(None, 'dp'), may hold values from 32.768 to 819.2
Outputs:
- block_output: bfloat16 [16384, 1024], P(('dp', 'tensor'))
- input_gradient: float32 [16384, 1024], P(('dp', 'tensor'))
- attention_entry_gradient: float32 [1024, 3, 1024], P('dp', None, 'tensor')
- attention_entry_updated: float32 [1024, 3, 1024], P('dp', None, 'tensor')
- attention_entry_momentum: float32 [1024, 3, 1024], P('dp', None, 'tensor')
- attention_entry_variance: float32 [1024, 3, 1024], P('dp', None, 'tensor')
- attention_exit_gradient: float32 [1024, 1024], P('tensor', 'dp')
- attention_exit_updated: float32 [1024, 1024], P('tensor', 'dp')
- attention_exit_momentum: float32 [1024, 1024], P('tensor', 'dp')
- attention_exit_variance: float32 [1024, 1024], P('tensor', 'dp')
- feedforward_entry_gradient: float32 [1024, 2, 2624], P('dp', None, 'tensor')
- feedforward_entry_updated: float32 [1024, 2, 2624], P('dp', None, 'tensor')
- feedforward_entry_momentum: float32 [1024, 2, 2624], P('dp', None, 'tensor')
- feedforward_entry_variance: float32 [1024, 2, 2624], P('dp', None, 'tensor')
- feedforward_exit_gradient: float32 [2624, 1024], P('tensor', 'dp')
- feedforward_exit_updated: float32 [2624, 1024], P('tensor', 'dp')
- feedforward_exit_momentum: float32 [2624, 1024], P('tensor', 'dp')
- feedforward_exit_variance: float32 [2624, 1024], P('tensor', 'dp')
- norm_gains_gradient: float32 [2, 1024], P(None, 'dp')
- norm_gains_updated: float32 [2, 1024], P(None, 'dp')
- norm_gains_momentum: float32 [2, 1024], P(None, 'dp')
- norm_gains_variance: float32 [2, 1024], P(None, 'dp')
- update_norms: float32 [5, 2], replicated
Inputs may be any that keep to these rules, and one draw needn't show every extreme that they name: `segment_ids`: each sequence of 1024 tokens is a pack of whole documents: its segment ids start at 0 at the sequence's first token and rise by one at each document's first token, so that a sequence of one-token documents reaches 1023. `positions`: counts from 0 at each document's first token and rises by one per token within the document; a document may fill a whole sequence.
All inputs are finite; a program needn't handle non-finite values.
Results may differ from a plain program's by a relative error of at most 0.012.
The roundings to bfloat16 on the way count: a program that leaves them out, or rounds other values in their place, can miss the bound.
Values may be sent and summed in bfloat16 or wider, within the bound.
No kernel may reach another device: no remote copies, remote signals or barrier semaphores. Data moves between devices by JAX's collectives and lax.ppermute only.
A program may use at most 192 MiB of HBM per device.

v0:
```python
import jax
import jax.numpy as jnp
from jax import lax
from jax.sharding import PartitionSpec as P

HD = 64
LEN = 1024


norm_eps = 1e-05
rope_base = 160000.0
masked_value = -1e30
beta_one = 0.9
beta_two = 0.95
adam_eps = 1e-06
decay_rate = 0.01
learn_rate = 0.3
ratio_eps = 1e-06


def layer_norm(values, gain_row):
    center = values - jnp.mean(values, axis=-1, keepdims=True)
    spread = jnp.mean(center * center, axis=-1, keepdims=True)
    return center * lax.rsqrt(spread + norm_eps) * gain_row


def rope_tables(places):
    half_dim = HD // 2
    frequency = rope_base ** (-(jnp.arange(half_dim, dtype=jnp.float32) * 2.0 / HD))
    angles = places.astype(jnp.float32)[:, None] * frequency[None, :]
    cosine = jnp.concatenate([jnp.cos(angles), jnp.cos(angles)], axis=-1)[:, None, :]
    sine_table = jnp.concatenate([jnp.sin(angles), jnp.sin(angles)], axis=-1)[:, None, :]
    return (cosine, sine_table)


def rotary(values, cosine, sine_table):
    half_dim = values.shape[-1] // 2
    turned = jnp.concatenate([-values[..., half_dim:], values[..., :half_dim]], axis=-1)
    return values * cosine + turned * sine_table


def geglu(gate_part, up_part):
    return jax.nn.gelu(gate_part, approximate=False) * up_part


def transpose_dot(first_arg, second_arg):
    return lax.dot_general(
        first_arg, second_arg, (((0,), (0,)), ((), ())), preferred_element_type=jnp.float32
    )


def dot_transposed(first_arg, second_arg):
    return lax.dot_general(
        first_arg, second_arg, (((1,), (1,)), ((), ())), preferred_element_type=jnp.float32
    )


def lamb_direction(master, gradient, momentum, variance):
    new_momentum = beta_one * momentum + (1.0 - beta_one) * gradient
    new_variance = beta_two * variance + (1.0 - beta_two) * gradient * gradient
    update = new_momentum / (jnp.sqrt(new_variance) + adam_eps) + decay_rate * master
    return (new_momentum, new_variance, update)


def per_device(
    tokens,
    cotangent,
    segment_ids,
    positions,
    attention_entry,
    attention_exit,
    feedforward_entry,
    feedforward_exit,
    norm_gains,
    momentum_attention_entry,
    momentum_attention_exit,
    momentum_feedforward_entry,
    momentum_feedforward_exit,
    momentum_norm_gains,
    variance_attention_entry,
    variance_attention_exit,
    variance_feedforward_entry,
    variance_feedforward_exit,
    variance_norm_gains,
):
    model_width = tokens.shape[1]
    group_rows = segment_ids.shape[0]
    slice_width = attention_exit.shape[0]
    hidden_slice = feedforward_exit.shape[0]
    head_count = slice_width // HD
    block_rows = min(512, LEN)
    sequence_count = group_rows // LEN
    block_count = group_rows // block_rows
    inner_blocks = LEN // block_rows
    scale_factor = HD ** (-0.5)
    copies = (
        lax.all_gather(attention_entry.astype(jnp.bfloat16), "dp", axis=0, tiled=True),
        lax.all_gather(attention_exit.astype(jnp.bfloat16), "dp", axis=1, tiled=True),
        lax.all_gather(feedforward_entry.astype(jnp.bfloat16), "dp", axis=0, tiled=True),
        lax.all_gather(feedforward_exit.astype(jnp.bfloat16), "dp", axis=1, tiled=True),
        lax.all_gather(norm_gains.astype(jnp.bfloat16), "dp", axis=1, tiled=True),
    )
    entry_copy, exit_copy, grow_copy, shrink_copy, gains_copy = copies
    gains_full = gains_copy.astype(jnp.float32)
    inputs = tokens.astype(jnp.float32)
    normed_one = layer_norm(inputs, gains_full[0]).astype(jnp.bfloat16)
    rows_one = lax.all_gather(normed_one, "tensor", axis=0, tiled=True)
    projected = jnp.dot(
        rows_one,
        entry_copy.reshape(model_width, 3 * slice_width),
        preferred_element_type=jnp.float32,
    ).reshape(group_rows, 3, head_count, HD)
    cosine, sine_table = rope_tables(positions)
    queries = rotary(projected[:, 0], cosine, sine_table).astype(jnp.bfloat16)
    key_rows = rotary(projected[:, 1], cosine, sine_table).astype(jnp.bfloat16)
    value_rows = projected[:, 2].astype(jnp.bfloat16)

    def block_scores(query_block, row_start, seq_start):
        key_block = lax.dynamic_slice_in_dim(key_rows, seq_start, LEN, 0)
        query_segments = lax.dynamic_slice_in_dim(segment_ids, row_start, block_rows, 0)
        key_segments = lax.dynamic_slice_in_dim(segment_ids, seq_start, LEN, 0)
        scores = (
            jnp.einsum("qhd,khd->hqk", query_block, key_block, preferred_element_type=jnp.float32)
            * scale_factor
        )
        allowed = (query_segments[:, None] == key_segments[None, :])[None]
        return (jnp.where(allowed, scores, masked_value), allowed)

    def attend_block(block_index):
        row_start = block_index * block_rows
        seq_start = row_start // LEN * LEN
        query_block = lax.dynamic_slice_in_dim(queries, row_start, block_rows, 0)
        scores, allowed = block_scores(query_block, row_start, seq_start)
        row_peak = jnp.max(scores, axis=-1, keepdims=True)
        exp_scores = jnp.exp(scores - row_peak)
        exp_total = jnp.sum(exp_scores, axis=-1, keepdims=True)
        probability = (exp_scores / exp_total).astype(jnp.bfloat16)
        value_block = lax.dynamic_slice_in_dim(value_rows, seq_start, LEN, 0)
        mixed = jnp.einsum(
            "hqk,khd->qhd", probability, value_block, preferred_element_type=jnp.float32
        )
        return (mixed.astype(jnp.bfloat16), (row_peak + jnp.log(exp_total))[..., 0])

    mixed_blocks, log_totals = lax.map(attend_block, jnp.arange(block_count))
    attended = mixed_blocks.reshape(group_rows, slice_width)
    branch = lax.psum_scatter(
        jnp.dot(attended, exit_copy, preferred_element_type=jnp.float32),
        "tensor",
        scatter_dimension=0,
        tiled=True,
    )
    hidden_state = inputs + branch
    normed_two = layer_norm(hidden_state, gains_full[1]).astype(jnp.bfloat16)
    rows_two = lax.all_gather(normed_two, "tensor", axis=0, tiled=True)
    gate_up = jnp.dot(
        rows_two,
        grow_copy.reshape(model_width, 2 * hidden_slice),
        preferred_element_type=jnp.float32,
    ).reshape(group_rows, 2, hidden_slice)
    activated = geglu(gate_up[:, 0], gate_up[:, 1]).astype(jnp.bfloat16)
    ffn_branch = lax.psum_scatter(
        jnp.dot(activated, shrink_copy, preferred_element_type=jnp.float32).astype(jnp.bfloat16),
        "tensor",
        scatter_dimension=0,
        tiled=True,
    ).astype(jnp.float32)
    block_output = (hidden_state + ffn_branch).astype(jnp.bfloat16)
    copies = (
        lax.all_gather(attention_entry.astype(jnp.bfloat16), "dp", axis=0, tiled=True),
        lax.all_gather(attention_exit.astype(jnp.bfloat16), "dp", axis=1, tiled=True),
        lax.all_gather(feedforward_entry.astype(jnp.bfloat16), "dp", axis=0, tiled=True),
        lax.all_gather(feedforward_exit.astype(jnp.bfloat16), "dp", axis=1, tiled=True),
        lax.all_gather(norm_gains.astype(jnp.bfloat16), "dp", axis=1, tiled=True),
    )
    entry_copy, exit_copy, grow_copy, shrink_copy, gains_copy = copies
    gains_full = gains_copy.astype(jnp.float32)
    out_rows = lax.all_gather(cotangent, "tensor", axis=0, tiled=True)
    grad_shrink = transpose_dot(activated, out_rows)
    grad_activated = dot_transposed(out_rows, shrink_copy)
    _, geglu_back = jax.vjp(geglu, gate_up[:, 0], gate_up[:, 1])
    grad_gate, grad_up = geglu_back(grad_activated)
    grad_gate_up = (
        jnp.stack([grad_gate, grad_up], axis=1)
        .astype(jnp.bfloat16)
        .reshape(group_rows, 2 * hidden_slice)
    )
    grad_grow = transpose_dot(rows_two, grad_gate_up)
    grow_flat = grow_copy.reshape(model_width, 2 * hidden_slice)
    grad_normed_two = lax.psum_scatter(
        dot_transposed(grad_gate_up, grow_flat), "tensor", scatter_dimension=0, tiled=True
    )
    _, norm_two_back = jax.vjp(layer_norm, hidden_state, gains_full[1])
    grad_hidden_norm, grad_gain_two = norm_two_back(grad_normed_two)
    grad_hidden = cotangent.astype(jnp.float32) + grad_hidden_norm
    hidden_rows = lax.all_gather(grad_hidden.astype(jnp.bfloat16), "tensor", axis=0, tiled=True)
    grad_exit = transpose_dot(attended, hidden_rows)
    grad_attended = (
        dot_transposed(hidden_rows, exit_copy)
        .astype(jnp.bfloat16)
        .reshape(group_rows, head_count, HD)
    )

    def sequence_back(sequence):
        seq_start = sequence * LEN
        key_block = lax.dynamic_slice_in_dim(key_rows, seq_start, LEN, 0)
        value_block = lax.dynamic_slice_in_dim(value_rows, seq_start, LEN, 0)

        def block_back(carried, inner_index):
            key_grad, value_grad = carried
            row_start = seq_start + inner_index * block_rows
            query_block = lax.dynamic_slice_in_dim(queries, row_start, block_rows, 0)
            grad_block = lax.dynamic_slice_in_dim(grad_attended, row_start, block_rows, 0)
            scores, allowed = block_scores(query_block, row_start, seq_start)
            log_block = lax.dynamic_index_in_dim(
                log_totals, row_start // block_rows, 0, keepdims=False
            )
            probability = jnp.where(allowed, jnp.exp(scores - log_block[..., None]), 0.0)
            grad_prob = jnp.einsum(
                "qhd,khd->hqk", grad_block, value_block, preferred_element_type=jnp.float32
            )
            inner_sum = jnp.sum(probability * grad_prob, axis=-1, keepdims=True)
            grad_scores = (probability * (grad_prob - inner_sum) * scale_factor).astype(
                jnp.bfloat16
            )
            query_grad = jnp.einsum(
                "hqk,khd->qhd", grad_scores, key_block, preferred_element_type=jnp.float32
            )
            key_grad = key_grad + jnp.einsum(
                "hqk,qhd->khd", grad_scores, query_block, preferred_element_type=jnp.float32
            )
            value_grad = value_grad + jnp.einsum(
                "hqk,qhd->khd",
                probability.astype(jnp.bfloat16),
                grad_block,
                preferred_element_type=jnp.float32,
            )
            return ((key_grad, value_grad), query_grad)

        zero_grad = jnp.zeros((LEN, head_count, HD), jnp.float32)
        (key_grad, value_grad), query_grads = lax.scan(
            block_back, (zero_grad, zero_grad), jnp.arange(inner_blocks)
        )
        return (query_grads.reshape(LEN, head_count, HD), key_grad, value_grad)

    query_grad_all, key_grad_all, value_grad_all = lax.map(
        sequence_back, jnp.arange(sequence_count)
    )

    def rotate_only(raw_rows):
        return rotary(raw_rows, cosine, sine_table)

    _, turn_back = jax.vjp(rotate_only, projected[:, 0])
    query_raw = turn_back(query_grad_all.reshape(group_rows, head_count, HD))[0]
    key_raw = turn_back(key_grad_all.reshape(group_rows, head_count, HD))[0]
    grad_projected = (
        jnp.stack([query_raw, key_raw, value_grad_all.reshape(group_rows, head_count, HD)], axis=1)
        .astype(jnp.bfloat16)
        .reshape(group_rows, 3 * slice_width)
    )
    grad_entry = transpose_dot(rows_one, grad_projected)
    entry_flat = entry_copy.reshape(model_width, 3 * slice_width)
    grad_normed_one = lax.psum_scatter(
        dot_transposed(grad_projected, entry_flat), "tensor", scatter_dimension=0, tiled=True
    )
    _, norm_one_back = jax.vjp(layer_norm, inputs, gains_full[0])
    grad_inputs_norm, grad_gain_one = norm_one_back(grad_normed_one)
    input_gradient = grad_hidden + grad_inputs_norm
    gains_local = jnp.stack([grad_gain_one, grad_gain_two])
    shards = (
        lax.psum_scatter(
            grad_entry.reshape(model_width, 3, slice_width), "dp", scatter_dimension=0, tiled=True
        ),
        lax.psum_scatter(grad_exit, "dp", scatter_dimension=1, tiled=True),
        lax.psum_scatter(
            grad_grow.reshape(model_width, 2, hidden_slice), "dp", scatter_dimension=0, tiled=True
        ),
        lax.psum_scatter(grad_shrink, "dp", scatter_dimension=1, tiled=True),
        lax.psum_scatter(gains_local, "dp", scatter_dimension=1, tiled=True),
    )
    gains_gradient = lax.psum(shards[4], "tensor")
    gradients = (shards[0], shards[1], shards[2], shards[3], gains_gradient)
    masters = (attention_entry, attention_exit, feedforward_entry, feedforward_exit, norm_gains)
    momenta = (
        momentum_attention_entry,
        momentum_attention_exit,
        momentum_feedforward_entry,
        momentum_feedforward_exit,
        momentum_norm_gains,
    )
    variances = (
        variance_attention_entry,
        variance_attention_exit,
        variance_feedforward_entry,
        variance_feedforward_exit,
        variance_norm_gains,
    )
    first_tensor = (lax.axis_index("tensor") == 0).astype(jnp.float32)
    shares = (1.0, 1.0, 1.0, 1.0, first_tensor)
    states = []
    square_rows = []
    for master, gradient, momentum, variance, share in zip(
        masters, gradients, momenta, variances, shares
    ):
        new_momentum, new_variance, update = lamb_direction(master, gradient, momentum, variance)
        states.append((new_momentum, new_variance, update))
        square_rows.append(jnp.stack([jnp.sum(master * master), jnp.sum(update * update)]) * share)
    totals = lax.psum(jnp.stack(square_rows), ("dp", "tensor"))
    updated_all = []
    for position_index in range(5):
        ratio = jnp.sqrt(totals[position_index, 0] / (totals[position_index, 1] + ratio_eps))
        updated_all.append(masters[position_index] - learn_rate * ratio * states[position_index][2])
    update_norms = jnp.sqrt(totals)
    return (
        block_output,
        input_gradient,
        gradients[0],
        updated_all[0],
        states[0][0],
        states[0][1],
        gradients[1],
        updated_all[1],
        states[1][0],
        states[1][1],
        gradients[2],
        updated_all[2],
        states[2][0],
        states[2][1],
        gradients[3],
        updated_all[3],
        states[3][0],
        states[3][1],
        gradients[4],
        updated_all[4],
        states[4][0],
        states[4][1],
        update_norms,
    )


def solution(mesh):
    in_specs = (
        P(("dp", "tensor"), None),
        P(("dp", "tensor"), None),
        P("dp"),
        P("dp"),
        P("dp", None, "tensor"),
        P("tensor", "dp"),
        P("dp", None, "tensor"),
        P("tensor", "dp"),
        P(None, "dp"),
        P("dp", None, "tensor"),
        P("tensor", "dp"),
        P("dp", None, "tensor"),
        P("tensor", "dp"),
        P(None, "dp"),
        P("dp", None, "tensor"),
        P("tensor", "dp"),
        P("dp", None, "tensor"),
        P("tensor", "dp"),
        P(None, "dp"),
    )
    out_specs = (
        P(("dp", "tensor"), None),
        P(("dp", "tensor"), None),
        P("dp", None, "tensor"),
        P("dp", None, "tensor"),
        P("dp", None, "tensor"),
        P("dp", None, "tensor"),
        P("tensor", "dp"),
        P("tensor", "dp"),
        P("tensor", "dp"),
        P("tensor", "dp"),
        P("dp", None, "tensor"),
        P("dp", None, "tensor"),
        P("dp", None, "tensor"),
        P("dp", None, "tensor"),
        P("tensor", "dp"),
        P("tensor", "dp"),
        P("tensor", "dp"),
        P("tensor", "dp"),
        P(None, "dp"),
        P(None, "dp"),
        P(None, "dp"),
        P(None, "dp"),
        P(),
    )
    return jax.shard_map(
        per_device, mesh=mesh, in_specs=in_specs, out_specs=out_specs, check_vma=False
    )
```

profile of v0, /device:TPU:0, one launch (start us, length us, event | category | flops | bytes accessed | tf_op | source)
XLA Modules:
  0.0 1250.2 jit_solution(15155489052560568349)
XLA Ops:
  10.5 22.3 %all_gather.32 = bf16[2,1024]{1,0:T(2,128)(2,1)S(1)} all-gather(bf16[2,128]{1,0:T(2,128)(2,1)S(1)} %get-tuple-element.764), channel_id=1, replica_groups=mesh['dp'=8,'tensor'=4] {'dp'}, dimensions={1}, use_global_device_ids=true | all-gather | bytes 4608 | tf_op jit(solution)/shard_map/all_gather | solution.py:101
  39.8 30.7 %all_gather.35 = bf16[256,1024]{1,0:T(8,128)(2,1)} all-gather(bf16[256,128]{1,0:T(8,128)(2,1)S(1)} %convert_element_type.129), channel_id=1, replica_groups=mesh['dp'=8,'tensor'=4] {'dp'}, dimensions={1}, use_global_device_ids=true | all-gather | bytes 589824 | tf_op jit(solution)/shard_map/all_gather | solution.py:98
  72.6 26.0 %all-gather.8.cloned.1.call-done = bf16[2048,1024]{1,0:T(8,128)(2,1)} async-done(((bf16[512,1024]{1,0:T(8,128)(2,1)}), bf16[2048,1024]{1,0:T(8,128)(2,1)}) %all-gather.8.cloned.1.call-update) | async-done | bytes 4194320 | tf_op jit(solution)/shard_map/all_gather | solution.py:107
  107.3 36.1 %while.61 = (s32[]{:T(128)}, bf16[4,512,4,64]{1,3,2,0:T(8,128)(2,1)}, f32[4,4,512]{2,1,0:T(4,128)S(1)}, s32[4]{0:T(128)S(1)}, bf16[2048,4,64]{0,2,1:T(8,128)(2,1...) while((s32[]{:T(128)}, ...), condition=%wide.region_5.6_spmd, body=%wide.region_2.5_spmd.sunk | while | flops 562690048 | bytes 28920236 | solution.py:144
  155.4 68.4 %reduce-scatter.12.cloned.1.call-done = f32[512,1024]{1,0:T(8,128)} async-done(((f32[2048,1024]{1,0:T(8,128)}), f32[512,1024]{1,0:T(8,128)}) %reduce-scatter.12.cloned.1.call-update) | async-done | bytes 2097168 | tf_op jit(solution)/shard_map/reduce_scatter | solution.py:146
  227.9 40.4 %all-gather.16.cloned.1.call-done = bf16[656,1024]{1,0:T(8,128)(2,1)} async-done(((bf16[656,128]{1,0:T(8,128)(2,1)}), bf16[656,1024]{1,0:T(8,128)(2,1)}) %all-gather.16.cloned.1.call-update) | async-done | bytes 1343504 | tf_op jit(solution)/shard_map/all_gather | solution.py:100
  268.3 34.1 %all-gather.18.cloned.1.call-done = bf16[2048,1024]{1,0:T(8,128)(2,1)} async-done(((bf16[512,1024]{1,0:T(8,128)(2,1)}), bf16[2048,1024]{1,0:T(8,128)(2,1)}) %all-gather.18.cloned.1.call-update) | async-done | bytes 4194320 | tf_op jit(solution)/shard_map/all_gather | solution.py:177
  310.2 51.8 %all-gather.14.cloned.1.call-done = bf16[1024,2,656]{0,2,1:T(8,128)(2,1)} async-done(((bf16[128,2,656]{0,2,1:T(8,128)(2,1)}), bf16[1024,2,656]{0,2,1:T(8,128)(2,1)}) %all-gather.14.cloned.1.call-update) | async-done | bytes 2686992 | tf_op jit(solution)/shard_map/all_gather | solution.py:99
  362.0 34.8 %all-gather.12.cloned.1.call-done = bf16[2048,1024]{1,0:T(8,128)(2,1)} async-done(((bf16[512,1024]{1,0:T(8,128)(2,1)}), bf16[2048,1024]{1,0:T(8,128)(2,1)}) %all-gather.12.cloned.1.call-update) | async-done | bytes 4194320 | tf_op jit(solution)/shard_map/all_gather | solution.py:154
  405.4 14.2 %fusion.66 = (bf16[2048,1,656]{0,2,1:T(8,128)(2,1)}, f32[2048,656]{0,1:T(8,128)}) fusion(f32[2048,656]{0,1:T(8,128)S(1)} %copy-done.6, f32[2048,2,656]{0,2,1:T(8,128)S(1)} %fusion.84), kind=kLoop, calls=%fused_computation.71 | loop fusion | flops 98074624 | bytes 24182784 | tf_op jit(solution)/shard_map/stack | solution.py:183
  454.5 56.4 %reduce-scatter.16.cloned.1.call-done = f32[512,1024]{1,0:T(8,128)} async-done(((f32[2048,1024]{1,0:T(8,128)}), f32[512,1024]{1,0:T(8,128)}) %reduce-scatter.16.cloned.1.call-update) | async-done | bytes 2097168 | tf_op jit(solution)/shard_map/reduce_scatter | solution.py:189
  513.8 44.3 %reduce-scatter.14.cloned.1.call-done = bf16[512,1024]{1,0:T(8,128)(2,1)} async-done(((bf16[2048,1024]{1,0:T(8,128)(2,1)}), bf16[512,1024]{1,0:T(8,128)(2,1)}) %reduce-scatter.14.cloned.1.call-update) | async-done | bytes 1048592 | tf_op jit(solution)/shard_map/reduce_scatter | solution.py:161
  582.9 16.0 %all-gather.20.cloned.1.call-done = bf16[2048,1024]{1,0:T(8,128)(2,1)} async-done(((bf16[512,1024]{1,0:T(8,128)(2,1)}), bf16[2048,1024]{1,0:T(8,128)(2,1)}) %all-gather.20.cloned.1.call-update) | async-done | bytes 4194320 | tf_op jit(solution)/shard_map/all_gather | solution.py:195
  603.4 260.1 %while.63 = (s32[]{:T(128)}, f32[2,1024,4,64]{3,2,1,0:T(4,128)}, f32[2,1024,4,64]{1,0,3,2:T(2,128)}, bf16[2,1024,4,64]{1,0,3,2:T(2,128)(2,1)}, s32[2]{0:T(128)S(...) while((s32[]{:T(128)}, f32[2,1024,4,64]{3,2,1,0:T(4,128)}, ...), condition=%wide.region_17.18_spmd, body=%wide.region_13.17_spmd.sunk | while | flops 1375213568 | bytes 152611856 | solution.py:245
  606.2 82.1 %while.64 = (s32[]{:T(128)}, f32[1024,4,64]{0,2,1:T(8,128)}, f32[1024,4,64]{0,2,1:T(8,128)S(1)}, f32[2,512,4,64]{1,3,2,0:T(8,128)S(1)}, s32[2]{0:T(128)S(1)}, /*...) while((s32[]{:T(128)}, f32[1024,4,64]{0,2,1:T(8,128)}, ...), condition=%wide.region_16.16_spmd.clone, body=%wide.region_14.15_spmd.clone.sunk | while | flops 1375213568 | bytes 134253072 | solution.py:240
  620.5 13.9 %fusion.183 = f32[1024,4,64]{0,2,1:T(8,128)} fusion(f32[4,512,1024]{2,1,0:T(8,128)} %copy-done, f32[4,512,1024]{2,1,0:T(8,128)} %fusion.182, f32[1024,4,64]{0,2,1:T(8,128)} %get-tuple-element.1027, pred[]{:T(512)S(6)} %compare.17, bf16[2048,4,64]{0,2,1:T(8,128)(2,1)} %get-tuple-element.1053, s32[]{:T(128)S(6)} %select_n.126), kind=kOutput, calls=%fused_computation.31.clone.1 | convolution fusion | flops 279448576 | bytes 35913732 | tf_op jit(solution)/shard_map/while/body/eval_jaxpr/while/body/eval_jaxpr/hqk,qhd->khd/dot_general | solution.py:228
  634.4 12.8 %fusion.185 = f32[2,512,4,64]{1,3,2,0:T(8,128)S(1)} fusion(f32[2,512,4,64]{1,3,2,0:T(8,128)S(1)} %get-tuple-element.1029, s32[]{:T(128)S(6)} %copy.121, bf16[1024,4,64]{0,2,1:T(8,128)(2,1)S(1)} %get-tuple-element.1056, f32[4,512,1024]{2,1,0:T(8,128)} %copy-done, f32[4,512,1024]{2,1,0:T(8,128)} %fusion.182), kind=kOutput, calls=%fused_computation.33.clone.1 | convolution fusion | flops 278924288 | bytes 34603012 | tf_op jit(solution)/shard_map/while/body/eval_jaxpr/while/body/eval_jaxpr/hqk,khd->qhd/dot_general | solution.py:225
  661.5 14.0 %fusion.183 = f32[1024,4,64]{0,2,1:T(8,128)} fusion(f32[4,512,1024]{2,1,0:T(8,128)} %copy-done, f32[4,512,1024]{2,1,0:T(8,128)} %fusion.182, f32[1024,4,64]{0,2,1:T(8,128)} %get-tuple-element.1027, pred[]{:T(512)S(6)} %compare.17, bf16[2048,4,64]{0,2,1:T(8,128)(2,1)} %get-tuple-element.1053, s32[]{:T(128)S(6)} %select_n.126), kind=kOutput, calls=%fused_computation.31.clone.1 | convolution fusion | flops 279448576 | bytes 35913732 | tf_op jit(solution)/shard_map/while/body/eval_jaxpr/while/body/eval_jaxpr/hqk,qhd->khd/dot_general | solution.py:228
  675.5 12.8 %fusion.185 = f32[2,512,4,64]{1,3,2,0:T(8,128)S(1)} fusion(f32[2,512,4,64]{1,3,2,0:T(8,128)S(1)} %get-tuple-element.1029, s32[]{:T(128)S(6)} %copy.121, bf16[1024,4,64]{0,2,1:T(8,128)(2,1)S(1)} %get-tuple-element.1056, f32[4,512,1024]{2,1,0:T(8,128)} %copy-done, f32[4,512,1024]{2,1,0:T(8,128)} %fusion.182), kind=kOutput, calls=%fused_computation.33.clone.1 | convolution fusion | flops 278924288 | bytes 34603012 | tf_op jit(solution)/shard_map/while/body/eval_jaxpr/while/body/eval_jaxpr/hqk,khd->qhd/dot_general | solution.py:225
  691.6 18.8 %dynamic_update_slice.55 = f32[2,1024,4,64]{1,0,3,2:T(2,128)} dynamic-update-slice(f32[2,1024,4,64]{1,0,3,2:T(2,128)} %get-tuple-element.1141, f32[1,1024,4,64]{1,0,3,2:T(1,128)S(1)} %copy.112, s32[]{:T(128)S(6)} %copy.145, s32[]{:T(128)} %constant.302.clone.1..sunk.1, s32[]{:T(128)} %constant.302.clone.1..sunk.1, s32[]{:T(128)} %constant.302.clone.1..sunk.1) | dynamic-update-slice | bytes 2097156 | tf_op jit(solution)/shard_map/while/body/jit(dynamic_update_index_in_dim)/dynamic_update_slice | solution.py:245
  714.4 17.8 %dynamic_update_slice.56 = bf16[2,1024,4,64]{1,0,3,2:T(2,128)(2,1)} dynamic-update-slice(bf16[2,1024,4,64]{1,0,3,2:T(2,128)(2,1)} %get-tuple-element.1142, bf16[1,1024,4,64]{1,0,3,2:T(2,128)(2,1)} %copy.113, s32[]{:T(128)S(6)} %copy.145, s32[]{:T(128)} %constant.302.clone.1..sunk.1, s32[]{:T(128)} %constant.302.clone.1..sunk.1, s32[]{:T(128)} %constant.302.clone.1..sunk.1) | dynamic-update-slice | bytes 1048580 | tf_op jit(solution)/shard_map/while/body/jit(dynamic_update_index_in_dim)/dynamic_update_slice | solution.py:245
  736.2 82.1 %while.64 = (s32[]{:T(128)}, f32[1024,4,64]{0,2,1:T(8,128)}, f32[1024,4,64]{0,2,1:T(8,128)S(1)}, f32[2,512,4,64]{1,3,2,0:T(8,128)S(1)}, s32[2]{0:T(128)S(1)}, /*...) while((s32[]{:T(128)}, f32[1024,4,64]{0,2,1:T(8,128)}, ...), condition=%wide.region_16.16_spmd.clone, body=%wide.region_14.15_spmd.clone.sunk | while | flops 1375213568 | bytes 134253072 | solution.py:240
  750.5 14.1 %fusion.183 = f32[1024,4,64]{0,2,1:T(8,128)} fusion(f32[4,512,1024]{2,1,0:T(8,128)} %copy-done, f32[4,512,1024]{2,1,0:T(8,128)} %fusion.182, f32[1024,4,64]{0,2,1:T(8,128)} %get-tuple-element.1027, pred[]{:T(512)S(6)} %compare.17, bf16[2048,4,64]{0,2,1:T(8,128)(2,1)} %get-tuple-element.1053, s32[]{:T(128)S(6)} %select_n.126), kind=kOutput, calls=%fused_computation.31.clone.1 | convolution fusion | flops 279448576 | bytes 35913732 | tf_op jit(solution)/shard_map/while/body/eval_jaxpr/while/body/eval_jaxpr/hqk,qhd->khd/dot_general | solution.py:228
  764.6 12.8 %fusion.185 = f32[2,512,4,64]{1,3,2,0:T(8,128)S(1)} fusion(f32[2,512,4,64]{1,3,2,0:T(8,128)S(1)} %get-tuple-element.1029, s32[]{:T(128)S(6)} %copy.121, bf16[1024,4,64]{0,2,1:T(8,128)(2,1)S(1)} %get-tuple-element.1056, f32[4,512,1024]{2,1,0:T(8,128)} %copy-done, f32[4,512,1024]{2,1,0:T(8,128)} %fusion.182), kind=kOutput, calls=%fused_computation.33.clone.1 | convolution fusion | flops 278924288 | bytes 34603012 | tf_op jit(solution)/shard_map/while/body/eval_jaxpr/while/body/eval_jaxpr/hqk,khd->qhd/dot_general | solution.py:225
  791.7 13.8 %fusion.183 = f32[1024,4,64]{0,2,1:T(8,128)} fusion(f32[4,512,1024]{2,1,0:T(8,128)} %copy-done, f32[4,512,1024]{2,1,0:T(8,128)} %fusion.182, f32[1024,4,64]{0,2,1:T(8,128)} %get-tuple-element.1027, pred[]{:T(512)S(6)} %compare.17, bf16[2048,4,64]{0,2,1:T(8,128)(2,1)} %get-tuple-element.1053, s32[]{:T(128)S(6)} %select_n.126), kind=kOutput, calls=%fused_computation.31.clone.1 | convolution fusion | flops 279448576 | bytes 35913732 | tf_op jit(solution)/shard_map/while/body/eval_jaxpr/while/body/eval_jaxpr/hqk,qhd->khd/dot_general | solution.py:228
  821.7 18.8 %dynamic_update_slice.55 = f32[2,1024,4,64]{1,0,3,2:T(2,128)} dynamic-update-slice(f32[2,1024,4,64]{1,0,3,2:T(2,128)} %get-tuple-element.1141, f32[1,1024,4,64]{1,0,3,2:T(1,128)S(1)} %copy.112, s32[]{:T(128)S(6)} %copy.145, s32[]{:T(128)} %constant.302.clone.1..sunk.1, s32[]{:T(128)} %constant.302.clone.1..sunk.1, s32[]{:T(128)} %constant.302.clone.1..sunk.1) | dynamic-update-slice | bytes 2097156 | tf_op jit(solution)/shard_map/while/body/jit(dynamic_update_index_in_dim)/dynamic_update_slice | solution.py:245
  844.3 17.8 %dynamic_update_slice.56 = bf16[2,1024,4,64]{1,0,3,2:T(2,128)(2,1)} dynamic-update-slice(bf16[2,1024,4,64]{1,0,3,2:T(2,128)(2,1)} %get-tuple-element.1142, bf16[1,1024,4,64]{1,0,3,2:T(2,128)(2,1)} %copy.113, s32[]{:T(128)S(6)} %copy.145, s32[]{:T(128)} %constant.302.clone.1..sunk.1, s32[]{:T(128)} %constant.302.clone.1..sunk.1, s32[]{:T(128)} %constant.302.clone.1..sunk.1) | dynamic-update-slice | bytes 1048580 | tf_op jit(solution)/shard_map/while/body/jit(dynamic_update_index_in_dim)/dynamic_update_slice | solution.py:245
  913.8 34.8 %reduce-scatter.22.cloned.1.call-done = f32[256,128]{1,0:T(8,128)} async-done(((f32[256,1024]{1,0:T(8,128)}), f32[256,128]{1,0:T(8,128)}) %reduce-scatter.22.cloned.1.call-update) | async-done | bytes 131088 | tf_op jit(solution)/shard_map/reduce_scatter | solution.py:273
  952.9 73.7 %reduce-scatter.20.cloned.1.call-done = f32[128,3,256]{2,0,1:T(8,128)} async-done(((f32[1024,3,256]{2,0,1:T(8,128)}), f32[128,3,256]{2,0,1:T(8,128)}) %reduce-scatter.20.cloned.1.call-update) | async-done | bytes 393232 | tf_op jit(solution)/shard_map/reduce_scatter | solution.py:270
  1032.9 66.6 %reduce-scatter.18.cloned.1.call-done = f32[512,1024]{1,0:T(8,128)} async-done(((f32[2048,1024]{1,0:T(8,128)}), f32[512,1024]{1,0:T(8,128)}) %reduce-scatter.18.cloned.1.call-update) | async-done | bytes 2097168 | tf_op jit(solution)/shard_map/reduce_scatter | solution.py:262
  1107.2 62.1 %reduce-scatter.28.cloned.1.call-done = f32[128,2]{1,0:T(8,128)} async-done(((f32[1024,2]{1,0:T(8,128)}), f32[128,2]{1,0:T(8,128)}) %reduce-scatter.28.cloned.1.call-update) | async-done | bytes 1040
  1185.3 40.5 %psum.15 = f32[5,2]{0,1:T(2,128)S(1)} all-reduce(f32[5,2]{0,1:T(2,128)} %stack.110), channel_id=1, replica_groups=mesh['dp'=8,'tensor'=4] {'dp','tensor'}, use_global_device_ids=true, to_apply=%region_39.40 | all-reduce | flops 10 | bytes 80 | tf_op jit(solution)/shard_map/psum | solution.py:307
  (317 shorter events, 336.9 us)
Async XLA Ops:
  7.2 32.6 %copy-start.47 = (s32[2048]{0:T(1024)S(1)}, s32[2048]{0:T(1024)}, u32[]{:S(2)}) copy-start(s32[2048]{0:T(1024)} %param.28) | copy-start | bytes 24580
  7.2 32.6 %copy-start.31 = (f32[256,128]{1,0:T(8,128)S(1)}, f32[256,128]{1,0:T(8,128)}, u32[]{:S(2)}) copy-start(f32[256,128]{1,0:T(8,128)} %param.30) | copy-start | bytes 393220
  7.2 65.4 %all-gather.10.cloned.1.call-start = ((), (), s32[]{:S(2)}) async-start(), calls=%async_computation.10 | async-start | bytes 1769472 | tf_op jit(solution)/shard_map/all_gather | solution.py:97
  9.1 89.5 %all-gather.8.cloned.1.call-start = ((), (), s32[]{:S(2)}) async-start(), calls=%async_computation.9 | async-start | bytes 5242880 | tf_op jit(solution)/shard_map/all_gather | solution.py:107
  39.7 184.1 %reduce-scatter.12.cloned.1.call-start = ((), (), s32[]{:S(2)}) async-start(), calls=%async_computation.11 | async-start | bytes 10485760 | tf_op jit(solution)/shard_map/reduce_scatter | solution.py:146
  152.2 71.6 %copy-start.2 = (bf16[512,1024]{1,0:T(8,128)(2,1)S(1)}, bf16[512,1024]{1,0:T(8,128)(2,1)}, u32[]{:S(2)}) copy-start(bf16[512,1024]{1,0:T(8,128)(2,1)} %param.25) | copy-start | bytes 3145732
  152.3 116.0 %all-gather.16.cloned.1.call-start = ((), (), s32[]{:S(2)}) async-start(), calls=%async_computation.14 | async-start | bytes 1511424 | tf_op jit(solution)/shard_map/all_gather | solution.py:100
  153.9 148.5 %all-gather.18.cloned.1.call-start = ((), (), s32[]{:S(2)}) async-start(), calls=%async_computation.16 | async-start | bytes 5242880 | tf_op jit(solution)/shard_map/all_gather | solution.py:177
  154.5 207.5 %all-gather.14.cloned.1.call-start = ((), (), s32[]{:S(2)}) async-start(), calls=%async_computation.13 | async-start | bytes 3022848 | tf_op jit(solution)/shard_map/all_gather | solution.py:99
  155.3 241.5 %all-gather.12.cloned.1.call-start = ((), (), s32[]{:S(2)}) async-start(), calls=%async_computation.12 | async-start | bytes 5242880 | tf_op jit(solution)/shard_map/all_gather | solution.py:154
  227.4 283.5 %reduce-scatter.16.cloned.1.call-start = ((), (), s32[]{:S(2)}) async-start(), calls=%async_computation.17 | async-start | bytes 10485760 | tf_op jit(solution)/shard_map/reduce_scatter | solution.py:189
  439.3 118.7 %reduce-scatter.14.cloned.1.call-start = ((), (), s32[]{:S(2)}) async-start(), calls=%async_computation.15 | async-start | bytes 5242880 | tf_op jit(solution)/shard_map/reduce_scatter | solution.py:161
  454.5 144.4 %all-gather.20.cloned.1.call-start = ((), (), s32[]{:S(2)}) async-start(), calls=%async_computation.18 | async-start | bytes 5242880 | tf_op jit(solution)/shard_map/all_gather | solution.py:195
  513.8 49.2 %copy-start.11 = (bf16[512,1024]{1,0:T(8,128)(2,1)S(1)}, bf16[512,1024]{1,0:T(8,128)(2,1)}, u32[]{:S(2)}) copy-start(bf16[512,1024]{1,0:T(8,128)(2,1)} %param.26) | copy-start | bytes 3145732
  564.3 338.2 %reduce-scatter.26.cloned.1.call-start = ((), (), s32[]{:S(2)}) async-start(), calls=%async_computation.23 | async-start | bytes 3022848 | tf_op jit(solution)/shard_map/reduce_scatter | solution.py:277
  572.0 336.3 %reduce-scatter.24.cloned.1.call-start = ((), (), s32[]{:S(2)}) async-start(), calls=%async_computation.22 | async-start | bytes 6045696 | tf_op jit(solution)/shard_map/reduce_scatter | solution.py:274
  582.8 16.1 %copy-start.29 = (bf16[256,1024]{1,0:T(8,128)(2,1)S(1)}, bf16[256,1024]{1,0:T(8,128)(2,1)}, u32[]{:S(2)}) copy-start(bf16[256,1024]{1,0:T(8,128)(2,1)} %all_gather.35) | copy-start | bytes 1572868
  582.8 365.8 %reduce-scatter.22.cloned.1.call-start = ((), (), s32[]{:S(2)}) async-start(), calls=%async_computation.21 | async-start | bytes 1179648 | tf_op jit(solution)/shard_map/reduce_scatter | solution.py:273
  883.8 142.8 %reduce-scatter.20.cloned.1.call-start = ((), (), s32[]{:S(2)}) async-start(), calls=%async_computation.20 | async-start | bytes 3538944 | tf_op jit(solution)/shard_map/reduce_scatter | solution.py:270
  895.1 204.4 %reduce-scatter.18.cloned.1.call-start = ((), (), s32[]{:S(2)}) async-start(), calls=%async_computation.19 | async-start | bytes 10485760 | tf_op jit(solution)/shard_map/reduce_scatter | solution.py:262
  902.3 46.3 %copy-start.32 = (f32[256,128]{1,0:T(8,128)S(1)}, f32[256,128]{1,0:T(8,128)}, u32[]{:S(2)}) copy-start(f32[256,128]{1,0:T(8,128)} %param.30) | copy-start | bytes 393220
  902.3 46.3 %copy-start.34 = (f32[256,128]{1,0:T(8,128)S(1)}, f32[256,128]{1,0:T(8,128)}, u32[]{:S(2)}) copy-start(f32[256,128]{1,0:T(8,128)} %param.40) | copy-start | bytes 393220
  902.3 46.3 %copy-start.35 = (f32[256,128]{1,0:T(8,128)S(1)}, f32[256,128]{1,0:T(8,128)}, u32[]{:S(2)}) copy-start(f32[256,128]{1,0:T(8,128)} %param.35) | copy-start | bytes 393220
  902.3 124.3 %copy-start.23 = (f32[128,3,256]{2,0,1:T(8,128)S(1)}, f32[128,3,256]{2,0,1:T(8,128)}, u32[]{:S(2)}) copy-start(f32[128,3,256]{2,0,1:T(8,128)} %param.29) | copy-start | bytes 1179652
  902.4 267.0 %reduce-scatter.28.cloned.1.call-start = ((), (), s32[]{:S(2)}) async-start(), calls=%async_computation.24 | async-start | bytes 589824
  902.4 197.1 %copy-start.3 = (bf16[512,1024]{1,0:T(8,128)(2,1)S(1)}, bf16[512,1024]{1,0:T(8,128)(2,1)}, u32[]{:S(2)}) copy-start(bf16[512,1024]{1,0:T(8,128)(2,1)} %param.25) | copy-start | bytes 3145732
  902.4 197.1 %copy-start.37 = (f32[1,1024]{1,0:T(1,128)S(1)}, f32[1,1024]{1,0:T(1,128)}, u32[]{:S(2)}) copy-start(f32[1,1024]{1,0:T(1,128)} %copy-done.36) | copy-start | bytes 12292
  902.4 197.1 %copy-start.39 = (f32[512]{0:T(512)S(1)}, f32[512]{0:T(512)}, u32[]{:S(2)}) copy-start(f32[512]{0:T(512)} %copy-done.38) | copy-start | bytes 6148
  908.3 193.3 %copy-start.45 = (f32[512]{0:T(512)S(1)}, f32[512]{0:T(512)}, u32[]{:S(2)}) copy-start(f32[512]{0:T(512)} %copy-done.44) | copy-start | bytes 6148
  908.3 193.3 %copy-start.41 = (f32[512]{0:T(512)S(1)}, f32[512]{0:T(512)}, u32[]{:S(2)}) copy-start(f32[512]{0:T(512)} %copy-done.40) | copy-start | bytes 6148
  1029.6 151.6 %copy-start.8 = (f32[512,1024]{1,0:T(8,128)S(1)}, f32[512,1024]{1,0:T(8,128)}, u32[]{:S(2)}) copy-start(f32[512,1024]{1,0:T(8,128)} %copy-done.7) | copy-start | bytes 6291460
  1181.1 52.5 %copy-start.46 = (f32[2,128]{1,0:T(2,128)S(1)}, f32[2,128]{1,0:T(2,128)}, u32[]{:S(2)}) copy-start(f32[2,128]{1,0:T(2,128)} %param.33) | copy-start | bytes 3076
  (38 other events, 145.0 us)
Sparse Core Ops, SparseCore 0:
  10.6 49.1 all-gather.9
  62.0 36.6 all-gather.7
  152.4 71.3 reduce-scatter.11
  226.3 41.9 all-gather.15
  269.7 32.6 all-gather.17
  304.8 57.1 all-gather.13
  364.2 32.6 all-gather.11
  439.4 71.4 reduce-scatter.15
  513.4 44.5 reduce-scatter.13
  564.4 34.4 all-gather.19
  603.0 73.1 reduce-scatter.25
  680.2 104.3 reduce-scatter.23
  883.9 64.6 reduce-scatter.21
  952.6 73.9 reduce-scatter.19
  1029.0 70.4 reduce-scatter.17
  1106.7 62.6 reduce-scatter.27
where the time goes:
time: 1270 us; the launch traced here: 1250 us
  waiting for transfers between devices  610 us (48%)
  matrix products  256 us (20%)
  local copies, waits for them, and re-layouts  138 us (11%)
  other arithmetic  116 us (9%)
  blocking collectives  99.9 us (8%)
  between operations  21.4 us (2%)
    dynamic_update_slice x10, local copies, waits for them, and re-layouts, per_device(): lax.map(sequence_back, jnp.arange(sequence_count))  84.6 us
    reduce_scatter x1, waiting for transfers between devices, per_device(): lax.psum_scatter(grad_entry.reshape(model_width, 3, slice_width), 'dp', s...  73.7 us
    reduce_scatter x1, waiting for transfers between devices, per_device(): lax.psum_scatter(jnp.dot(attended, exit_copy, preferred_element_type=jnp....  68.4 us
    reduce_scatter x1, waiting for transfers between devices, per_device(): lax.psum_scatter(dot_transposed(grad_projected, entry_flat), 'tensor', sc...  66.6 us
    unnamed x17, waiting for transfers between devices  62.9 us
    reduce_scatter x1, waiting for transfers between devices, per_device(): lax.psum_scatter(dot_transposed(grad_gate_up, grow_flat), 'tensor', scatt...  56.4 us
    dot_general x4, matrix products, block_back(): jnp.einsum('hqk,qhd->khd', grad_scores, query_block, preferred_element_ty...  55.8 us
    all_gather x1, waiting for transfers between devices, per_device(): lax.all_gather(feedforward_entry.astype(jnp.bfloat16), 'dp', axis=0, tile...  51.8 us
  transfers between devices with their start and end apart: 16, of which 13 were waited for; matrix products, arithmetic and copies ran while one was open for 29% of the time, Pallas kernels for 0%

commit v1 on v0

v1 whole, which is shorter than its diff:
```python
import jax
import jax.numpy as jnp
from jax import lax
from jax.experimental import pallas as pl
from jax.experimental.pallas import tpu as pltpu
from jax.sharding import PartitionSpec as P

HD = 64
LEN = 1024
HALF = HD // 2
PAIR = 2 * HD

norm_eps = 1e-05
rope_base = 160000.0
masked_value = -1e30
beta_one = 0.9
beta_two = 0.95
adam_eps = 1e-06
decay_rate = 0.01
learn_rate = 0.3
ratio_eps = 1e-06
score_scale = HD ** (-0.5)
root_half = 0.7071067811865476
root_two_pi = 0.3989422804014327

bf16 = jnp.bfloat16
f32 = jnp.float32
VMEM_LIMIT = 60 * 1024 * 1024


def dot_nn(a, b):
    return lax.dot_general(a, b, (((1,), (0,)), ((), ())), preferred_element_type=f32)


def dot_nt(a, b):
    return lax.dot_general(a, b, (((1,), (1,)), ((), ())), preferred_element_type=f32)


def dot_tn(a, b):
    return lax.dot_general(a, b, (((0,), (0,)), ((), ())), preferred_element_type=f32)


def exchange(value, axis, bit):
    size = lax.axis_size(axis)
    return lax.ppermute(value, axis, [(i, i ^ bit) for i in range(size)])


def swap_core(value):
    return exchange(value, "tensor", 1)


def upper_bits(size):
    return [1 << k for k in range(1, size.bit_length() - 1)]


def gather_stages(color):
    dp = lax.axis_size("dp")
    last = [("dp", 1), ("tensor", 2)]
    return [("dp", b) for b in upper_bits(dp)] + (last if color == 0 else last[::-1])


def gather_rows(part, color):
    held = part[None]
    for axis, bit in gather_stages(color):
        other = exchange(held, axis, bit)
        held = jnp.concatenate([held, other], axis=2 if axis == "dp" else 0)
    return held


def scatter_rows(full, color):
    held = full
    stages = gather_stages(color)[::-1]
    for index, (axis, bit) in enumerate(stages):
        if axis == "dp":
            half = held.shape[2] // 2
            keep, send = held[:, :, :half], held[:, :, half:]
        else:
            keep, send = held[:1], held[1:]
        got = exchange(send, axis, bit)
        held = keep.astype(f32) + got.astype(f32)
        if index < len(stages) - 1:
            held = held.astype(bf16)
    return held[0]


def relative_columns(value):
    dp = lax.axis_size("dp")
    rows, width = value.shape
    bits = dp.bit_length() - 1
    index = lax.axis_index("dp")
    cube = value.reshape((rows,) + (2,) * bits + (width // dp,))
    for k in range(bits):
        axis = 1 + (bits - 1 - k)
        cube = jnp.where((index >> k) & 1 == 1, jnp.flip(cube, axis), cube)
    order = (0, bits) + tuple(range(1, bits)) + (bits + 1,)
    return cube.transpose(order).reshape(rows, width)


def absolute_columns(value):
    dp = lax.axis_size("dp")
    rows, width = value.shape
    bits = dp.bit_length() - 1
    index = lax.axis_index("dp")
    cube = value.reshape((rows,) + (2,) * bits + (width // dp,))
    order = (0,) + tuple(range(2, bits + 1)) + (1, bits + 1)
    cube = cube.transpose(order)
    for k in range(bits):
        axis = 1 + (bits - 1 - k)
        cube = jnp.where((index >> k) & 1 == 1, jnp.flip(cube, axis), cube)
    return cube.reshape(rows, width)


def tree_sum(value, axis):
    size = lax.axis_size(axis)
    if size > 8:
        bit = 1
        while bit < size:
            value = value + exchange(value, axis, bit)
            bit *= 2
        return value
    terms = [value] + [exchange(value, axis, b) for b in range(1, size)]
    while len(terms) > 1:
        terms = [terms[i] + terms[i + 1] for i in range(0, len(terms), 2)]
    return terms[0]


def score_bias(segr_ref, segc_ref, bias_ref):
    bias_ref[...] = jnp.where(segc_ref[...] == segr_ref[...], 0.0, masked_value)


QB = 256


def attend_kernel(n1_ref, w_ref, cos_ref, sin_ref, segr_ref, segc_ref, qkv_ref, o_ref, lse_ref, bias_ref):
    @pl.when(pl.program_id(0) == 0)
    def _():
        score_bias(segr_ref, segc_ref, bias_ref)

    projected = dot_nt(w_ref[0], n1_ref[...])
    cosine, sine = cos_ref[...], sin_ref[...]

    def turned(rows):
        low, high = rows[:HALF], rows[HALF:]
        return jnp.concatenate([low * cosine - high * sine, high * cosine + low * sine], axis=0)

    for head in range(2):
        at = head * HD
        query = turned(projected[at : at + HD]).astype(bf16) * jnp.asarray(score_scale, bf16)
        key = turned(projected[PAIR + at : PAIR + at + HD])
        value = projected[2 * PAIR + at : 2 * PAIR + at + HD].astype(bf16)
        qkv_ref[0, at : at + HD] = query
        qkv_ref[0, PAIR + at : PAIR + at + HD] = key.astype(bf16)
        qkv_ref[0, 2 * PAIR + at : 2 * PAIR + at + HD] = value
        key_rows = key.T.astype(bf16)
        for block in range(LEN // QB):
            span = slice(block * QB, (block + 1) * QB)
            scores = dot_nn(key_rows, query[:, span]) + bias_ref[:, span]
            peak = jnp.max(scores, axis=0, keepdims=True)
            weight = jnp.exp(scores - peak)
            total = jnp.sum(weight, axis=0, keepdims=True)
            mixed = dot_nn(value, weight.astype(bf16)) / total
            o_ref[0, at : at + HD, span] = mixed.astype(bf16)
            lse_ref[0, head : head + 1, span] = peak + jnp.log(total)


def whole(shape):
    return pl.BlockSpec(shape, lambda i: (0,) * len(shape))


def leading(shape):
    return pl.BlockSpec((1,) + shape[1:], lambda i: (i,) + (0,) * (len(shape) - 1))


def attend(n1, w_entry, cosine, sine, seg_row, seg_col):
    pairs = w_entry.shape[0]
    width = n1.shape[1]
    return pl.pallas_call(
        attend_kernel,
        name="attend",
        grid=(pairs,),
        in_specs=[
            whole(n1.shape),
            leading(w_entry.shape),
            whole(cosine.shape),
            whole(sine.shape),
            whole(seg_row.shape),
            whole(seg_col.shape),
        ],
        out_specs=[
            leading((pairs, 3 * PAIR, LEN)),
            leading((pairs, PAIR, LEN)),
            leading((pairs, 2, LEN)),
        ],
        out_shape=[
            jax.ShapeDtypeStruct((pairs, 3 * PAIR, LEN), bf16),
            jax.ShapeDtypeStruct((pairs, PAIR, LEN), bf16),
            jax.ShapeDtypeStruct((pairs, 2, LEN), f32),
        ],
        scratch_shapes=[pltpu.VMEM((LEN, LEN), f32)],
        compiler_params=pltpu.CompilerParams(vmem_limit_bytes=VMEM_LIMIT),
        cost_estimate=pl.CostEstimate(
            flops=pairs * (2 * 3 * PAIR * width * LEN + 4 * 4 * PAIR * LEN * LEN),
            bytes_accessed=pairs * 4 * PAIR * LEN * 4,
            transcendentals=pairs * 2 * LEN * LEN,
        ),
    )(n1, w_entry, cosine, sine, seg_row, seg_col)


def attend_back_kernel(
    x_ref, dh_ref, qkv_ref, o_ref, lse_ref, cos_ref, sin_ref, segr_ref, segc_ref, dp_ref, bias_ref
):
    @pl.when(pl.program_id(0) == 0)
    def _():
        score_bias(segr_ref, segc_ref, bias_ref)

    cosine, sine = cos_ref[...], sin_ref[...]
    grad_mixed = dot_nt(x_ref[0], dh_ref[...]).astype(bf16)

    def turned_back(rows):
        low, high = rows[:HALF], rows[HALF:]
        return jnp.concatenate([low * cosine + high * sine, high * cosine - low * sine], axis=0)

    for head in range(2):
        at = head * HD
        query = qkv_ref[0, at : at + HD]
        key = qkv_ref[0, PAIR + at : PAIR + at + HD]
        value = qkv_ref[0, 2 * PAIR + at : 2 * PAIR + at + HD]
        grad_out = grad_mixed[at : at + HD]
        mixed = o_ref[0, at : at + HD].astype(f32)
        inner = jnp.sum(mixed * grad_out.astype(f32), axis=0, keepdims=True)
        key_rows = key.astype(f32).T.astype(bf16)
        value_rows = value.astype(f32).T.astype(bf16)
        query_grads = []
        key_grad = jnp.zeros((HD, LEN), f32)
        value_grad = jnp.zeros((HD, LEN), f32)
        for block in range(LEN // QB):
            span = slice(block * QB, (block + 1) * QB)
            scores = dot_nn(key_rows, query[:, span]) + bias_ref[:, span]
            weight = jnp.exp(scores - lse_ref[0, head : head + 1, span])
            grad_weight = dot_nn(value_rows, grad_out[:, span])
            grad_scores = (weight * (grad_weight - inner[:, span])).astype(bf16)
            query_grads.append(dot_nn(key, grad_scores))
            key_grad += dot_nt(query[:, span], grad_scores)
            value_grad += dot_nt(grad_out[:, span], weight.astype(bf16))
        query_grad = jnp.concatenate(query_grads, axis=1) * score_scale
        dp_ref[0, at : at + HD] = turned_back(query_grad).astype(bf16)
        dp_ref[0, PAIR + at : PAIR + at + HD] = turned_back(key_grad).astype(bf16)
        dp_ref[0, 2 * PAIR + at : 2 * PAIR + at + HD] = value_grad.astype(bf16)


def attend_back(w_exit, dh, qkv, mixed, lse, cosine, sine, seg_row, seg_col):
    pairs = w_exit.shape[0]
    width = dh.shape[1]
    return pl.pallas_call(
        attend_back_kernel,
        name="attend_back",
        grid=(pairs,),
        in_specs=[
            leading(w_exit.shape),
            whole(dh.shape),
            leading(qkv.shape),
            leading(mixed.shape),
            leading(lse.shape),
            whole(cosine.shape),
            whole(sine.shape),
            whole(seg_row.shape),
            whole(seg_col.shape),
        ],
        out_specs=leading(qkv.shape),
        out_shape=jax.ShapeDtypeStruct(qkv.shape, bf16),
        scratch_shapes=[pltpu.VMEM((LEN, LEN), f32)],
        compiler_params=pltpu.CompilerParams(vmem_limit_bytes=VMEM_LIMIT),
        cost_estimate=pl.CostEstimate(
            flops=pairs * (2 * PAIR * width * LEN + 10 * 4 * PAIR * LEN * LEN),
            bytes_accessed=pairs * 8 * PAIR * LEN * 2,
            transcendentals=pairs * 2 * LEN * LEN,
        ),
    )(w_exit, dh, qkv, mixed, lse, cosine, sine, seg_row, seg_col)


def row_spans(rows, most):
    pieces = -(-rows // most)
    step = -(-rows // pieces // 16) * 16
    return [(at, min(rows, at + step)) for at in range(0, rows, step)]


def feed_kernel(n2_ref, c_ref, w_ref, out_ref, dn_ref, dw_ref, out_acc, dn_acc):
    step = pl.program_id(0)

    @pl.when(step == 0)
    def _():
        out_acc[...] = jnp.zeros_like(out_acc)
        dn_acc[...] = jnp.zeros_like(dn_acc)

    hidden = w_ref.shape[2]
    n2, cot = n2_ref[...], c_ref[...]
    for lo, hi in row_spans(hidden, 336):
        w_gate, w_up, w_down = w_ref[0, 0, lo:hi], w_ref[0, 1, lo:hi], w_ref[0, 2, lo:hi]
        gate, up, grad_act = dot_nt(w_gate, n2), dot_nt(w_up, n2), dot_nt(w_down, cot)
        phi = 0.5 + 0.5 * lax.erf(gate * root_half)
        density = jnp.exp(-0.5 * gate * gate) * root_two_pi
        gelu = gate * phi
        active = (gelu * up).astype(bf16)
        grad_gate = (grad_act * up * (phi + gate * density)).astype(bf16)
        grad_up = (grad_act * gelu).astype(bf16)
        dw_ref[0, 0, lo:hi] = dot_nn(grad_gate, n2).astype(bf16)
        dw_ref[0, 1, lo:hi] = dot_nn(grad_up, n2).astype(bf16)
        dw_ref[0, 2, lo:hi] = dot_nn(active, cot).astype(bf16)
        out_acc[...] += dot_tn(active, w_down)
        dn_acc[...] += dot_tn(grad_gate, w_gate) + dot_tn(grad_up, w_up)

    @pl.when(step == pl.num_programs(0) - 1)
    def _():
        out_ref[...] = out_acc[...].astype(bf16)
        dn_ref[...] = dn_acc[...].astype(bf16)


def feed(n2, cot, weights):
    shape = n2.shape
    rows, width = shape
    hidden = weights.shape[2] * weights.shape[0]
    return pl.pallas_call(
        feed_kernel,
        name="feed",
        grid=(weights.shape[0],),
        in_specs=[whole(shape), whole(shape), leading(weights.shape)],
        out_specs=[whole(shape), whole(shape), leading(weights.shape)],
        out_shape=[
            jax.ShapeDtypeStruct(shape, bf16),
            jax.ShapeDtypeStruct(shape, bf16),
            jax.ShapeDtypeStruct(weights.shape, bf16),
        ],
        scratch_shapes=[pltpu.VMEM(shape, f32), pltpu.VMEM(shape, f32)],
        compiler_params=pltpu.CompilerParams(vmem_limit_bytes=VMEM_LIMIT),
        cost_estimate=pl.CostEstimate(
            flops=18 * rows * width * hidden,
            bytes_accessed=4 * rows * width * 2 + 12 * width * hidden,
            transcendentals=2 * rows * hidden,
        ),
    )(n2, cot, weights)


def norm_stats(values):
    center = values - jnp.mean(values, axis=-1, keepdims=True)
    spread = jnp.mean(center * center, axis=-1, keepdims=True)
    rate = lax.rsqrt(spread + norm_eps)
    return center * rate, rate


def norm_back(scaled, rate, gain, upstream):
    weighted = upstream * gain
    grad = rate * (
        weighted
        - jnp.mean(weighted, axis=-1, keepdims=True)
        - scaled * jnp.mean(weighted * scaled, axis=-1, keepdims=True)
    )
    return grad, jnp.sum(upstream * scaled, axis=0)


def rope_tables(places):
    frequency = rope_base ** (-(jnp.arange(HALF, dtype=f32) * 2.0 / HD))
    angles = frequency[:, None] * places.astype(f32)[None, :]
    return jnp.cos(angles), jnp.sin(angles)


def lamb_direction(master, gradient, momentum, variance):
    new_momentum = beta_one * momentum + (1.0 - beta_one) * gradient
    new_variance = beta_two * variance + (1.0 - beta_two) * gradient * gradient
    update = new_momentum / (jnp.sqrt(new_variance) + adam_eps) + decay_rate * master
    return (new_momentum, new_variance, update)


def per_device(
    tokens,
    cotangent,
    segment_ids,
    positions,
    attention_entry,
    attention_exit,
    feedforward_entry,
    feedforward_exit,
    norm_gains,
    momentum_attention_entry,
    momentum_attention_exit,
    momentum_feedforward_entry,
    momentum_feedforward_exit,
    momentum_norm_gains,
    variance_attention_entry,
    variance_attention_exit,
    variance_feedforward_entry,
    variance_feedforward_exit,
    variance_norm_gains,
):
    own, width = tokens.shape
    local = attention_entry.shape[0]
    slice_width = attention_exit.shape[0]
    hidden = feedforward_exit.shape[0]
    pairs = slice_width // PAIR
    tensor_size = lax.axis_size("tensor")
    assert tensor_size == 4 and own * 2 == LEN and segment_ids.shape[0] == 2 * LEN and pairs == 2

    entry_rows = (
        attention_entry.astype(bf16)
        .reshape(local, 3, pairs, PAIR)
        .transpose(2, 1, 3, 0)
        .reshape(pairs, 3 * PAIR, local)
    )
    exit_rows = attention_exit.astype(bf16).reshape(pairs, PAIR, local)
    feed_rows = jnp.concatenate(
        [
            feedforward_entry.astype(bf16).transpose(1, 2, 0).reshape(2 * hidden, local),
            feedforward_exit.astype(bf16),
        ],
        axis=0,
    )
    gains_held = norm_gains.astype(bf16)
    for axis, bit in gather_stages(0):
        if axis == "dp":
            gains_held = jnp.concatenate([gains_held, exchange(gains_held, axis, bit)], axis=1)
    gains = gains_held.astype(f32)

    w_entry = [gather_rows(entry_rows[p], p) for p in range(pairs)]
    w_exit = [gather_rows(exit_rows[p], p) for p in range(pairs)]
    spans = row_spans(3 * hidden, 512)
    w_feed = [gather_rows(feed_rows[lo:hi], k % 2) for k, (lo, hi) in enumerate(spans)]

    inputs = relative_columns(tokens).astype(f32)
    cot_own = relative_columns(cotangent)
    cot = jnp.concatenate([cot_own, swap_core(cot_own)], axis=0)
    lane = lax.axis_index("tensor")

    def rows_of(vector):
        first = lax.dynamic_slice_in_dim(vector, lane * own, own, 0)
        second = lax.dynamic_slice_in_dim(vector, (lane ^ 1) * own, own, 0)
        return jnp.concatenate([first, second])

    segments = rows_of(segment_ids)
    seg_row, seg_col = segments[None, :], segments[:, None]
    cosine, sine = rope_tables(rows_of(positions))

    scaled_one, rate_one = norm_stats(inputs)
    normed = (scaled_one * gains[0]).astype(bf16)
    n1 = jnp.concatenate([normed, swap_core(normed)], axis=0)
    entry_full = jnp.stack(w_entry, axis=1).reshape(2 * pairs, 3 * PAIR, width)
    exit_full = jnp.stack(w_exit, axis=1).reshape(2 * pairs, PAIR, width)
    qkv, mixed, lse = attend(n1, entry_full, cosine, sine, seg_row, seg_col)
    mixed_flat = mixed.reshape(2 * pairs * PAIR, LEN)
    branch = dot_tn(mixed_flat, exit_full.reshape(2 * pairs * PAIR, width))
    hidden_state = inputs + branch[:own] + swap_core(branch[own:].astype(bf16)).astype(f32)
    scaled_two, rate_two = norm_stats(hidden_state)
    normed_two = (scaled_two * gains[1]).astype(bf16)
    n2 = jnp.concatenate([normed_two, swap_core(normed_two)], axis=0)
    feed_full = jnp.concatenate(w_feed, axis=1).reshape(2, 3, hidden, width)
    out_part, dn_part, feed_grad = feed(n2, cot, feed_full)
    block_output = absolute_columns(
        (hidden_state + out_part[:own].astype(f32) + swap_core(out_part[own:]).astype(f32)).astype(bf16)
    )

    feed_flat = feed_grad.reshape(2, 3 * hidden, width)
    g_feed = [scatter_rows(feed_flat[:, lo:hi], k % 2) for k, (lo, hi) in enumerate(spans)]
    dn2 = dn_part[:own].astype(f32) + swap_core(dn_part[own:]).astype(f32)
    norm_grad, gain_two = norm_back(scaled_two, rate_two, gains[1], dn2)
    grad_hidden = cot_own.astype(f32) + norm_grad
    dh_own = grad_hidden.astype(bf16)
    dh = jnp.concatenate([dh_own, swap_core(dh_own)], axis=0)
    exit_grad = dot_nn(mixed_flat, dh).astype(bf16).reshape(2, pairs, PAIR, width)
    g_exit = [scatter_rows(exit_grad[:, p], p) for p in range(pairs)]
    dproj = attend_back(exit_full, dh, qkv, mixed, lse, cosine, sine, seg_row, seg_col)
    dproj_flat = dproj.reshape(2 * pairs * 3 * PAIR, LEN)
    entry_grad = dot_nn(dproj_flat, n1).astype(bf16).reshape(2, pairs, 3 * PAIR, width)
    g_entry = [scatter_rows(entry_grad[:, p], p) for p in range(pairs)]
    dn1_part = dot_tn(dproj_flat, entry_full.reshape(2 * pairs * 3 * PAIR, width))
    dn1 = dn1_part[:own] + swap_core(dn1_part[own:].astype(bf16)).astype(f32)
    norm_grad_one, gain_one = norm_back(scaled_one, rate_one, gains[0], dn1)
    input_gradient = absolute_columns(grad_hidden + norm_grad_one)

    gains_local = jnp.stack([gain_one, gain_two])
    for axis, bit in gather_stages(0)[::-1]:
        if axis == "dp":
            half = gains_local.shape[1] // 2
            gains_local = gains_local[:, :half] + exchange(gains_local[:, half:], axis, bit)
    gains_gradient = tree_sum(gains_local, "tensor")
    entry_gradient = (
        jnp.stack(g_entry).reshape(pairs, 3, PAIR, local).transpose(3, 1, 0, 2).reshape(local, 3, slice_width)
    )
    exit_gradient = jnp.concatenate(g_exit, axis=0)
    feed_gradient = jnp.concatenate(g_feed, axis=0)
    grow_gradient = feed_gradient[: 2 * hidden].reshape(2, hidden, local).transpose(2, 0, 1)
    shrink_gradient = feed_gradient[2 * hidden :]
    gradients = (entry_gradient, exit_gradient, grow_gradient, shrink_gradient, gains_gradient)

    masters = (attention_entry, attention_exit, feedforward_entry, feedforward_exit, norm_gains)
    momenta = (
        momentum_attention_entry,
        momentum_attention_exit,
        momentum_feedforward_entry,
        momentum_feedforward_exit,
        momentum_norm_gains,
    )
    variances = (
        variance_attention_entry,
        variance_attention_exit,
        variance_feedforward_entry,
        variance_feedforward_exit,
        variance_norm_gains,
    )
    first_tensor = (lane == 0).astype(f32)
    shares = (1.0, 1.0, 1.0, 1.0, first_tensor)
    states = []
    square_rows = []
    for master, gradient, momentum, variance, share in zip(masters, gradients, momenta, variances, shares):
        new_momentum, new_variance, update = lamb_direction(master, gradient, momentum, variance)
        states.append((new_momentum, new_variance, update))
        square_rows.append(jnp.stack([jnp.sum(master * master), jnp.sum(update * update)]) * share)
    totals = tree_sum(tree_sum(jnp.stack(square_rows), "tensor"), "dp")
    updated_all = []
    for index in range(5):
        ratio = jnp.sqrt(totals[index, 0] / (totals[index, 1] + ratio_eps))
        updated_all.append(masters[index] - learn_rate * ratio * states[index][2])
    outputs = [block_output, input_gradient]
    for index in range(5):
        outputs += [gradients[index], updated_all[index], states[index][0], states[index][1]]
    return tuple(outputs + [jnp.sqrt(totals)])


def solution(mesh):
    rows = P(("dp", "tensor"), None)
    first = P("dp", None, "tensor")
    second = P("tensor", "dp")
    gains = P(None, "dp")
    weights = (first, second, first, second, gains)
    in_specs = (rows, rows, P("dp"), P("dp")) + weights * 3
    out_specs = (rows, rows) + tuple(spec for spec in weights for _ in range(4)) + (P(),)
    return jax.shard_map(per_device, mesh=mesh, in_specs=in_specs, out_specs=out_specs, check_vma=False)
```

time: 1270 us -> 689 us (0.54)
  waiting for transfers between devices: 610 us -> 189 us
  matrix products: 256 us -> 16 us
  starting transfers between devices: 1.3 us -> 115 us
  blocking collectives: 99.9 us -> 0 us
  Pallas kernels: 0 us -> 99.6 us
  local copies, waits for them, and re-layouts: 138 us -> 90.3 us
  other arithmetic: 116 us -> 158 us
    reduce_scatter x8 -> x0, waiting for transfers between devices: 344 us -> none  [the longest x1 73.7 us: per_device(): lax.psum_scatter(grad_entry.reshape(model_width, 3, slice_width), 'dp', s...]
    dot_general x40 -> x4, matrix products: 256 us -> 16 us  [the longest x2 9.29 us: dot_tn(): lax.dot_general(a, b, (((0,), (0,)), ((), ())), preferred_element_type=f32)]
    all_gather x7 -> x0, waiting for transfers between devices: 203 us -> none  [the longest x1 51.8 us: per_device(): lax.all_gather(feedforward_entry.astype(jnp.bfloat16), 'dp', axis=0, tile...]
    ppermute x0 -> x91, waiting for transfers between devices: none -> 189 us  [exchange(): return lax.ppermute(value, axis, [(i, i ^ bit) for i in range(size)])]
    ppermute x0 -> x91, starting transfers between devices: none -> 115 us  [exchange(): return lax.ppermute(value, axis, [(i, i ^ bit) for i in range(size)])]
    pallas_call x0 -> x3, Pallas kernels: none -> 99.6 us  [the longest x1 39 us: feed(): pl.pallas_call(feed_kernel, name='feed', grid=(weights.shape[0],), in_spe...]
    dynamic_update_slice x10 -> x0, local copies, waits for them, and re-layouts: 84.6 us -> none  [per_device(): lax.map(sequence_back, jnp.arange(sequence_count))]
    unnamed x17 -> x0, waiting for transfers between devices: 62.9 us -> none
  transfers between devices with their start and end apart: 16 -> 91, of which waited for: 13 -> 37; matrix products, arithmetic and copies ran while one was open for 29% -> 35% of each run, Pallas kernels for 0% -> 9%
where the time goes in v1:
time: 689 us; the launch traced here: 678 us
  waiting for transfers between devices  189 us (27%)
  other arithmetic  158 us (23%)
  starting transfers between devices  115 us (17%)
  Pallas kernels  99.6 us (14%)
  local copies, waits for them, and re-layouts  90.3 us (13%)
  matrix products  16 us (2%)
  between operations  9.09 us (1%)
    ppermute x91, waiting for transfers between devices, exchange(): return lax.ppermute(value, axis, [(i, i ^ bit) for i in range(size)])  189 us
    ppermute x91, starting transfers between devices, exchange(): return lax.ppermute(value, axis, [(i, i ^ bit) for i in range(size)])  115 us
    pallas_call x1, Pallas kernels, feed(): pl.pallas_call(feed_kernel, name='feed', grid=(weights.shape[0],), in_spe...  39 us
    pallas_call x1, Pallas kernels, attend_back(): pl.pallas_call(attend_back_kernel, name='attend_back', grid=(pairs,), in_...  30.9 us
    concatenate x1, other arithmetic, per_device(): feed_full = jnp.concatenate(w_feed, axis=1).reshape(2, 3, hidden, width)  29.8 us
    pallas_call x1, Pallas kernels, attend(): pl.pallas_call(attend_kernel, name='attend', grid=(pairs,), in_specs=[who...  29.7 us
    rev x2, local copies, waits for them, and re-layouts, absolute_columns(): cube = jnp.where(index >> k & 1 == 1, jnp.flip(cube, axis), cube)  21.3 us
    convert_element_type x23, other arithmetic, scatter_rows(): held = held.astype(bf16)  20.1 us
  transfers between devices with their start and end apart: 91, of which 37 were waited for; matrix products, arithmetic and copies ran while one was open for 35% of the time, Pallas kernels for 9%

profile of v1, /device:TPU:0, one launch (start us, length us, event | category | flops | bytes accessed | tf_op | source)
XLA Modules:
  0.0 678.0 jit_solution(69329587231720787)
XLA Ops:
  21.0 7.6 %rev.43 = bf16[512,2,2,2,128]{4,2,1,3,0:T(2,128)(2,1)} reverse(bf16[512,2,2,2,128]{4,2,1,3,0:T(2,128)(2,1)S(1)} %get-tuple-element.151), dimensions={2} | reverse | bytes 2097152 | tf_op jit(solution)/shard_map/jit(_flip)/rev | solution.py:94
  34.0 5.5 rev.46
  41.7 7.8 %fusion.1 = f32[512]{0:T(512)S(1)} fusion(f32[512]{0:T(512)S(1)} %broadcast_multiply_fusion.5, bf16[512,2,2,2,128]{4,2,1,3,0:T(2,128)(2,1)S(1)} %broadcast_select_fusion.6, pred[]{:T(512)S(6)} %eq.8), kind=kLoop, calls=%fused_computation.9 | loop fusion | flops 2620928 | bytes 1052673 | tf_op jit(solution)/shard_map/reduce_sum | solution.py:345
  77.5 3.3 collective-permute-start.31
  92.5 11.8 %collective-permute-done.9 = bf16[1,384,256]{2,1,0:T(8,128)(2,1)S(1)} collective-permute-done((bf16[1,384,256]{2,1,0:T(8,128)(2,1)S(1)}, bf16[1,384,256]{2,1,0:T(8,128)(2,1)S(1)}, u32[]{:S(2)}, u32[]{:S(2)}) %collective-permute-start.9) | collective-permute-done | bytes 196640 | tf_op jit(solution)/shard_map/ppermute | solution.py:45
  105.3 8.5 %collective-permute-done.5 = bf16[1,384,256]{2,1,0:T(8,128)(2,1)S(1)} collective-permute-done((bf16[1,384,256]{2,1,0:T(8,128)(2,1)S(1)}, bf16[1,384,256]{2,1,0:T(8,128)(2,1)S(1)}, u32[]{:S(2)}, u32[]{:S(2)}) %collective-permute-start.5) | collective-permute-done | bytes 196640 | tf_op jit(solution)/shard_map/ppermute | solution.py:45
  139.9 4.7 collective-permute-done.11
  151.6 29.7 %attend.1 = (bf16[4,384,1024]{2,1,0:T(8,128)(2,1)}, bf16[4,128,1024]{2,1,0:T(8,128)(2,1)}, f32[4,2,1024]{2,1,0:T(2,128)}) custom-call(bf16[1024,1024]{1,0:T(8,128)(2,1)} %pad_maximum_fusion.1.n1_ref, bf16[4,384,1024]{2,1,0:T(8,128)(2,1)} %bitcast.133, f32[32,1024]{1,0:T(8,128)} %get-tuple-element.135.cos_ref, f32[32,1024]{1,0:T(8,128)} %get-tuple-element.134.sin_ref, ...), custom_call_target="tpu_custom_call" | custom-call | flops 11811160064 | bytes 8388608 | tf_op jit(solution)/shard_map/attend/pallas_call | solution.py:177
  190.7 8.9 %collective-permute-done.33 = bf16[1,496,512]{2,1,0:T(8,128)(2,1)S(1)} collective-permute-done((bf16[1,496,512]{2,1,0:T(8,128)(2,1)S(1)}, bf16[1,496,512]{2,1,0:T(8,128)(2,1)S(1)}, u32[]{:S(2)}, u32[]{:S(2)}) %collective-permute-start.33) | collective-permute-done | bytes 507936 | tf_op jit(solution)/shard_map/ppermute | solution.py:45
  208.0 12.7 %collective-permute-done.38 = bf16[2,480,512]{2,1,0:T(8,128)(2,1)S(1)} collective-permute-done((bf16[2,480,512]{2,1,0:T(8,128)(2,1)S(1)}, bf16[2,480,512]{2,1,0:T(8,128)(2,1)S(1)}, u32[]{:S(2)}, u32[]{:S(2)}) %collective-permute-start.38) | collective-permute-done | bytes 983072 | tf_op jit(solution)/shard_map/ppermute | solution.py:45
  220.7 4.3 collective-permute-done.26
  224.9 18.8 %collective-permute-done.34 = bf16[1,496,1024]{2,1,0:T(8,128)(2,1)S(1)} collective-permute-done((bf16[1,496,1024]{2,1,0:T(8,128)(2,1)S(1)}, bf16[1,496,1024]{2,1,0:T(8,128)(2,1)S(1)}, u32[]{:S(2)}, u32[]{:S(2)}) %collective-permute-start.34) | collective-permute-done | bytes 1015840 | tf_op jit(solution)/shard_map/ppermute | solution.py:45
  243.7 29.8 %maximum_maximum_fusion = bf16[2,1968,1024]{2,1,0:T(8,128)(2,1)} fusion(bf16[2,480,512]{2,1,0:T(8,128)(2,1)} %copy-done.49, bf16[1,480,512]{2,1,0:T(8,128)(2,1)} %collective-permute-done.37, bf16[1,480,256]{2,1,0:T(8,128)(2,1)S(1)} %copy-done.30, bf16[1,480,128]{2,1,0:T(8,128)(2,1)} %collective-permute-done.35, bf16[1,480,128]{2,1,0:T(8,128)(2,1)} %slice_bitcast_fusion.8, ...), kind=kLoop, calls=%fused_computation | loop fusion | flops 161218560 | bytes 16121856 | tf_op jit(solution)/shard_map/concatenate | solution.py:453
  275.1 39.0 %feed.1 = (bf16[1024,1024]{1,0:T(8,128)(2,1)}, bf16[1024,1024]{1,0:T(8,128)(2,1)}, bf16[2,3,656,1024]{3,2,1,0:T(8,128)(2,1)}) custom-call(bf16[1024,1024]{1,0:T(8,128)(2,1)} %pad_maximum_fusion.2.n2_ref, bf16[1024,1024]{1,0:T(8,128)(2,1)} %pad_maximum_fusion.3.c_ref, bf16[2,3,656,1024]{3,2,1,0:T(8,128)(2,1)} %bitcast.130), custom_call_target="tpu_custom_call" | custom-call | flops 24763170816 | bytes 24510464 | tf_op jit(solution)/shard_map/feed/pallas_call | solution.py:322
  328.1 13.3 %collective-permute-done.71 = bf16[2,480,512]{2,1,0:T(8,128)(2,1)} collective-permute-done((bf16[2,480,512]{2,1,0:T(8,128)(2,1)}, bf16[2,480,512]{2,1,0:T(8,128)(2,1)}, u32[]{:S(2)}, u32[]{:S(2)}) %collective-permute-start.71) | collective-permute-done | bytes 983072 | tf_op jit(solution)/shard_map/ppermute | solution.py:45
  344.0 15.4 %collective-permute-done.63 = bf16[2,496,512]{2,1,0:T(8,128)(2,1)} collective-permute-done((bf16[2,496,512]{2,1,0:T(8,128)(2,1)}, bf16[2,496,512]{2,1,0:T(8,128)(2,1)}, u32[]{:S(2)}, u32[]{:S(2)}) %collective-permute-start.63) | collective-permute-done | bytes 1015840 | tf_op jit(solution)/shard_map/ppermute | solution.py:45
  364.1 7.0 %collective-permute-done.67 = bf16[1,496,1024]{2,1,0:T(8,128)(2,1)} collective-permute-done((bf16[1,496,1024]{2,1,0:T(8,128)(2,1)}, bf16[1,496,1024]{2,1,0:T(8,128)(2,1)}, u32[]{:S(2)}, u32[]{:S(2)}) %collective-permute-start.67) | collective-permute-done | bytes 1015840 | tf_op jit(solution)/shard_map/ppermute | solution.py:45
  381.0 3.8 fusion.22
  388.6 10.3 %rev.49 = bf16[512,2,2,2,128]{4,2,1,3,0:T(2,128)(2,1)} reverse(bf16[512,2,2,2,128]{4,2,1,3,0:T(2,128)(2,1)} %broadcast_select_fusion), dimensions={2} | reverse | bytes 2097152 | tf_op jit(solution)/shard_map/jit(_flip)/rev | solution.py:109
  415.9 19.5 %collective-permute-start.74 = (bf16[1,480,128]{2,1,0:T(8,128)(2,1)S(1)}, bf16[1,480,128]{2,1,0:T(8,128)(2,1)S(1)}, u32[]{:S(2)}, u32[]{:S(2)}) collective-permute-start(bf16[1,480,128]{2,1,0:T(8,128)(2,1)S(1)} %slice.536), channel_id=1, source_target_pairs={{0,8},{4,12},{8,0},{12,4},{16,24},{20,28},{24,16},{28,20},{1,9},{5... | collective-permute-start | bytes 368648 | tf_op jit(solution)/shard_map/ppermute | solution.py:45
  435.4 7.5 %collective-permute-done.65 = bf16[1,496,256]{2,1,0:T(8,128)(2,1)S(1)} collective-permute-done((bf16[1,496,256]{2,1,0:T(8,128)(2,1)S(1)}, bf16[1,496,256]{2,1,0:T(8,128)(2,1)S(1)}, u32[]{:S(2)}, u32[]{:S(2)}) %collective-permute-start.65) | collective-permute-done | bytes 253984 | tf_op jit(solution)/shard_map/ppermute | solution.py:45
  443.7 4.7 collective-permute-done.69
  448.5 4.7 collective-permute-done.61
  454.4 5.4 collective-permute-done.70
  479.9 30.9 %attend_back.1 = bf16[4,384,1024]{2,1,0:T(8,128)(2,1)} custom-call(bf16[4,128,1024]{2,1,0:T(8,128)(2,1)} %bitcast.132, bf16[1024,1024]{1,0:T(8,128)(2,1)} %pad_maximum_fusion.4.dh_ref, bf16[4,384,1024]{2,1,0:T(8,128)(2,1)} %get-tuple-element.32.qkv_ref, bf16[4,128,1024]{2,1,0:T(8,128)(2,1)} %get-tuple-element.29.o_ref, ...), custom_call_target="tpu_custom_call" | custom-call | flops 22548578304 | bytes 8388608 | tf_op jit(solution)/shard_map/attend_back/pallas_call | solution.py:254
  510.9 6.5 fusion.32
  517.4 3.7 convolution_convert_fusion
  531.4 14.9 %collective-permute-done.52 = bf16[1,128,512]{2,1,0:T(8,128)(2,1)S(1)} collective-permute-done((bf16[1,128,512]{2,1,0:T(8,128)(2,1)S(1)}, bf16[1,128,512]{2,1,0:T(8,128)(2,1)S(1)}, u32[]{:S(2)}, u32[]{:S(2)}) %collective-permute-start.52) | collective-permute-done | bytes 131104 | tf_op jit(solution)/shard_map/ppermute | solution.py:45
  574.1 3.3 multiply_add_fusion
  587.4 11.0 %rev.52 = f32[512,2,2,2,128]{4,2,1,3,0:T(2,128)} reverse(f32[512,2,2,2,128]{4,2,1,3,0:T(2,128)} %reverse_select_fusion.1), dimensions={2} | reverse | bytes 4194304 | tf_op jit(solution)/shard_map/jit(_flip)/rev | solution.py:109
  618.7 12.9 %collective-permute-done.45 = bf16[1,384,256]{2,1,0:T(8,128)(2,1)S(1)} collective-permute-done((bf16[1,384,256]{2,1,0:T(8,128)(2,1)S(1)}, bf16[1,384,256]{2,1,0:T(8,128)(2,1)S(1)}, u32[]{:S(2)}, u32[]{:S(2)}) %collective-permute-start.45) | collective-permute-done | bytes 196640 | tf_op jit(solution)/shard_map/ppermute | solution.py:45
  654.3 3.3 collective-permute-start.87
  (508 shorter events, 298.6 us)
Async XLA Ops:
  2.1 48.8 %collective-permute-start = (bf16[2,128]{1,0:T(2,128)(2,1)S(1)}, bf16[2,128]{1,0:T(2,128)(2,1)S(1)}, u32[]{:S(2)}, u32[]{:S(2)}) collective-permute-start(bf16[2,128]{1,0:T(2,128)(2,1)S(1)} %get-tuple-element.147), channel_id=1, source_target_pairs={{0,8},{4,12},{8,0},{12,4},{16,24},{20,28},{24,16},{28,20},{1,9},{5... | collective-permute-start | bytes 1544 | tf_op jit(solution)/shard_map/ppermute | solution.py:45
  6.7 59.8 %collective-permute-start.12 = (bf16[1,128,128]{2,1,0:T(8,128)(2,1)}, bf16[1,128,128]{2,1,0:T(8,128)(2,1)}, u32[]{:S(2)}, u32[]{:S(2)}) collective-permute-start(bf16[1,128,128]{2,1,0:T(8,128)(2,1)} %get-tuple-element.126), channel_id=1, source_target_pairs={{0,8},{4,12},{8,0},{12,4},{16,24},{20,28},{24,16},{28,20},{1,9},{5... | collective-permute-start | bytes 98312 | tf_op jit(solution)/shard_map/ppermute | solution.py:45
  6.7 58.6 %collective-permute-start.16 = (bf16[1,128,128]{2,1,0:T(8,128)(2,1)}, bf16[1,128,128]{2,1,0:T(8,128)(2,1)}, u32[]{:S(2)}, u32[]{:S(2)}) collective-permute-start(bf16[1,128,128]{2,1,0:T(8,128)(2,1)} %get-tuple-element.127), channel_id=1, source_target_pairs={{0,8},{4,12},{8,0},{12,4},{16,24},{20,28},{24,16},{28,20},{1,9},{5... | collective-permute-start | bytes 98312 | tf_op jit(solution)/shard_map/ppermute | solution.py:45
  10.4 72.4 %collective-permute-start.35 = (bf16[1,480,128]{2,1,0:T(8,128)(2,1)}, bf16[1,480,128]{2,1,0:T(8,128)(2,1)}, u32[]{:S(2)}, u32[]{:S(2)}) collective-permute-start(bf16[1,480,128]{2,1,0:T(8,128)(2,1)} %slice_bitcast_fusion.8), channel_id=1, source_target_pairs={{0,8},{4,12},{8,0},{12,4},{16,24},{20,28},{24,16},{28,20},{1,9},{5... | collective-permute-start | bytes 368648 | tf_op jit(solution)/shard_map/ppermute | solution.py:45
  13.3 68.5 %collective-permute-start.8 = (bf16[1,384,128]{2,1,0:T(8,128)(2,1)}, bf16[1,384,128]{2,1,0:T(8,128)(2,1)}, u32[]{:S(2)}, u32[]{:S(2)}) collective-permute-start(bf16[1,384,128]{2,1,0:T(8,128)(2,1)} %bitcast.5), channel_id=1, source_target_pairs={{0,8},{4,12},{8,0},{12,4},{16,24},{20,28},{24,16},{28,20},{1,9},{5... | collective-permute-start | bytes 294920 | tf_op jit(solution)/shard_map/ppermute | solution.py:45
  81.8 53.7 %collective-permute-start.3 = (bf16[512,1024]{1,0:T(8,128)(2,1)S(1)}, bf16[512,1024]{1,0:T(8,128)(2,1)S(1)}, u32[]{:S(2)}, u32[]{:S(2)}) collective-permute-start(bf16[512,1024]{1,0:T(8,128)(2,1)S(1)} %multiply_convert_fusion.1), channel_id=1, source_target_pairs={{0,1},{1,0},{2,3},{3,2},{4,5},{5,4},{6,7},{7,6},{8,9},{9,8},{10,11... | collective-permute-start | bytes 3145736 | tf_op jit(solution)/shard_map/ppermute | solution.py:45
  131.8 71.1 %collective-permute-start.22 = (bf16[512,1024]{1,0:T(8,128)(2,1)S(1)}, bf16[512,1024]{1,0:T(8,128)(2,1)}, u32[]{:S(2)}, u32[]{:S(2)}) collective-permute-start(bf16[512,1024]{1,0:T(8,128)(2,1)S(1)} %reshape.279), channel_id=1, source_target_pairs={{0,1},{1,0},{2,3},{3,2},{4,5},{5,4},{6,7},{7,6},{8,9},{9,8},{10,11... | collective-permute-start | bytes 3145736 | tf_op jit(solution)/shard_map/ppermute | solution.py:45
  133.6 50.8 %collective-permute-start.32 = (bf16[1,496,256]{2,1,0:T(8,128)(2,1)}, bf16[1,496,256]{2,1,0:T(8,128)(2,1)S(1)}, u32[]{:S(2)}, u32[]{:S(2)}) collective-permute-start(bf16[1,496,256]{2,1,0:T(8,128)(2,1)} %pad_maximum_fusion.26), channel_id=1, source_target_pairs={{0,16},{4,20},{8,24},{12,28},{16,0},{20,4},{24,8},{28,12},{1,17},{... | collective-permute-start | bytes 761864 | tf_op jit(solution)/shard_map/ppermute | solution.py:45
  135.5 49.6 %collective-permute-start.28 = (bf16[1,496,256]{2,1,0:T(8,128)(2,1)}, bf16[1,496,256]{2,1,0:T(8,128)(2,1)}, u32[]{:S(2)}, u32[]{:S(2)}) collective-permute-start(bf16[1,496,256]{2,1,0:T(8,128)(2,1)} %pad_maximum_fusion.25), channel_id=1, source_target_pairs={{0,16},{4,20},{8,24},{12,28},{16,0},{20,4},{24,8},{28,12},{1,17},{... | collective-permute-start | bytes 761864 | tf_op jit(solution)/shard_map/ppermute | solution.py:45
  144.7 42.0 %collective-permute-start.37 = (bf16[1,480,512]{2,1,0:T(8,128)(2,1)}, bf16[1,480,512]{2,1,0:T(8,128)(2,1)}, u32[]{:S(2)}, u32[]{:S(2)}) collective-permute-start(bf16[1,480,512]{2,1,0:T(8,128)(2,1)} %pad_maximum_fusion.17), channel_id=1, source_target_pairs={{0,2},{1,3},{2,0},{3,1},{4,6},{5,7},{6,4},{7,5},{8,10},{9,11},{10,... | collective-permute-start | bytes 1474568 | tf_op jit(solution)/shard_map/ppermute | solution.py:45
  147.9 40.0 %collective-permute-start.25 = (bf16[1,496,512]{2,1,0:T(8,128)(2,1)}, bf16[1,496,512]{2,1,0:T(8,128)(2,1)}, u32[]{:S(2)}, u32[]{:S(2)}) collective-permute-start(bf16[1,496,512]{2,1,0:T(8,128)(2,1)} %pad_maximum_fusion.14), channel_id=1, source_target_pairs={{0,4},{4,0},{8,12},{12,8},{16,20},{20,16},{24,28},{28,24},{1,5},{5... | collective-permute-start | bytes 1523720 | tf_op jit(solution)/shard_map/ppermute | solution.py:45
  199.9 43.9 %collective-permute-start.34 = (bf16[1,496,1024]{2,1,0:T(8,128)(2,1)S(1)}, bf16[1,496,1024]{2,1,0:T(8,128)(2,1)S(1)}, u32[]{:S(2)}, u32[]{:S(2)}) collective-permute-start(bf16[1,496,1024]{2,1,0:T(8,128)(2,1)S(1)} %pad_maximum_fusion.8), channel_id=1, source_target_pairs={{0,2},{1,3},{2,0},{3,1},{4,6},{5,7},{6,4},{7,5},{8,10},{9,11},{10,... | collective-permute-start | bytes 3047432 | tf_op jit(solution)/shard_map/ppermute | solution.py:45
  202.9 40.8 %collective-permute-start.30 = (bf16[2,496,512]{2,1,0:T(8,128)(2,1)S(1)}, bf16[2,496,512]{2,1,0:T(8,128)(2,1)}, u32[]{:S(2)}, u32[]{:S(2)}) collective-permute-start(bf16[2,496,512]{2,1,0:T(8,128)(2,1)S(1)} %pad_maximum_fusion.7), channel_id=1, source_target_pairs={{0,4},{4,0},{8,12},{12,8},{16,20},{20,16},{24,28},{28,24},{1,5},{5... | collective-permute-start | bytes 3047432 | tf_op jit(solution)/shard_map/ppermute | solution.py:45
  208.0 65.5 %collective-permute-start.21 = (bf16[512,1024]{1,0:T(8,128)(2,1)S(1)}, bf16[512,1024]{1,0:T(8,128)(2,1)S(1)}, u32[]{:S(2)}, u32[]{:S(2)}) collective-permute-start(bf16[512,1024]{1,0:T(8,128)(2,1)S(1)} %multiply_convert_fusion), channel_id=1, source_target_pairs={{0,1},{1,0},{2,3},{3,2},{4,5},{5,4},{6,7},{7,6},{8,9},{9,8},{10,11... | collective-permute-start | bytes 3145736 | tf_op jit(solution)/shard_map/ppermute | solution.py:45
  319.9 39.5 %collective-permute-start.63 = (bf16[2,496,512]{2,1,0:T(8,128)(2,1)}, bf16[2,496,512]{2,1,0:T(8,128)(2,1)}, u32[]{:S(2)}, u32[]{:S(2)}) collective-permute-start(bf16[2,496,512]{2,1,0:T(8,128)(2,1)} %slice.514), channel_id=1, source_target_pairs={{0,4},{4,0},{8,12},{12,8},{16,20},{20,16},{24,28},{28,24},{1,5},{5... | collective-permute-start | bytes 3047432 | tf_op jit(solution)/shard_map/ppermute | solution.py:45
  323.7 38.9 %collective-permute-start.59 = (bf16[1,496,1024]{2,1,0:T(8,128)(2,1)}, bf16[1,496,1024]{2,1,0:T(8,128)(2,1)}, u32[]{:S(2)}, u32[]{:S(2)}) collective-permute-start(bf16[1,496,1024]{2,1,0:T(8,128)(2,1)} %get-tuple-element.118), channel_id=1, source_target_pairs={{0,2},{1,3},{2,0},{3,1},{4,6},{5,7},{6,4},{7,5},{8,10},{9,11},{10,... | collective-permute-start | bytes 3047432 | tf_op jit(solution)/shard_map/ppermute | solution.py:45
  324.0 47.1 %collective-permute-start.67 = (bf16[1,496,1024]{2,1,0:T(8,128)(2,1)}, bf16[1,496,1024]{2,1,0:T(8,128)(2,1)}, u32[]{:S(2)}, u32[]{:S(2)}) collective-permute-start(bf16[1,496,1024]{2,1,0:T(8,128)(2,1)} %get-tuple-element.119), channel_id=1, source_target_pairs={{0,2},{1,3},{2,0},{3,1},{4,6},{5,7},{6,4},{7,5},{8,10},{9,11},{10,... | collective-permute-start | bytes 3047432 | tf_op jit(solution)/shard_map/ppermute | solution.py:45
  326.8 50.5 %collective-permute-start.40 = (bf16[512,1024]{1,0:T(8,128)(2,1)}, bf16[512,1024]{1,0:T(8,128)(2,1)}, u32[]{:S(2)}, u32[]{:S(2)}) collective-permute-start(bf16[512,1024]{1,0:T(8,128)(2,1)} %slice.369), channel_id=1, source_target_pairs={{0,1},{1,0},{2,3},{3,2},{4,5},{5,4},{6,7},{7,6},{8,9},{9,8},{10,11... | collective-permute-start | bytes 3145736 | tf_op jit(solution)/shard_map/ppermute | solution.py:45
  341.4 39.6 %collective-permute-start.39 = (bf16[512,1024]{1,0:T(8,128)(2,1)S(1)}, bf16[512,1024]{1,0:T(8,128)(2,1)S(1)}, u32[]{:S(2)}, u32[]{:S(2)}) collective-permute-start(bf16[512,1024]{1,0:T(8,128)(2,1)S(1)} %slice.367), channel_id=1, source_target_pairs={{0,1},{1,0},{2,3},{3,2},{4,5},{5,4},{6,7},{7,6},{8,9},{9,8},{10,11... | collective-permute-start | bytes 3145736 | tf_op jit(solution)/shard_map/ppermute | solution.py:45
  359.4 45.1 %collective-permute-start.72 = (bf16[1,480,512]{2,1,0:T(8,128)(2,1)}, bf16[1,480,512]{2,1,0:T(8,128)(2,1)}, u32[]{:S(2)}, u32[]{:S(2)}) collective-permute-start(bf16[1,480,512]{2,1,0:T(8,128)(2,1)} %slice.532), channel_id=1, source_target_pairs={{0,2},{1,3},{2,0},{3,1},{4,6},{5,7},{6,4},{7,5},{8,10},{9,11},{10,... | collective-permute-start | bytes 1474568 | tf_op jit(solution)/shard_map/ppermute | solution.py:45
  362.7 43.4 %collective-permute-start.64 = (bf16[1,496,512]{2,1,0:T(8,128)(2,1)}, bf16[1,496,512]{2,1,0:T(8,128)(2,1)}, u32[]{:S(2)}, u32[]{:S(2)}) collective-permute-start(bf16[1,496,512]{2,1,0:T(8,128)(2,1)} %slice.516), channel_id=1, source_target_pairs={{0,2},{1,3},{2,0},{3,1},{4,6},{5,7},{6,4},{7,5},{8,10},{9,11},{10,... | collective-permute-start | bytes 1523720 | tf_op jit(solution)/shard_map/ppermute | solution.py:45
  404.5 66.2 %collective-permute-start.41 = (bf16[512,1024]{1,0:T(8,128)(2,1)}, bf16[512,1024]{1,0:T(8,128)(2,1)}, u32[]{:S(2)}, u32[]{:S(2)}) collective-permute-start(bf16[512,1024]{1,0:T(8,128)(2,1)} %get-tuple-element.112), channel_id=1, source_target_pairs={{0,1},{1,0},{2,3},{3,2},{4,5},{5,4},{6,7},{7,6},{8,9},{9,8},{10,11... | collective-permute-start | bytes 3145736 | tf_op jit(solution)/shard_map/ppermute | solution.py:45
  411.5 36.9 %collective-permute-start.69 = (bf16[1,496,256]{2,1,0:T(8,128)(2,1)S(1)}, bf16[1,496,256]{2,1,0:T(8,128)(2,1)S(1)}, u32[]{:S(2)}, u32[]{:S(2)}) collective-permute-start(bf16[1,496,256]{2,1,0:T(8,128)(2,1)S(1)} %slice.526), channel_id=1, source_target_pairs={{0,16},{4,20},{8,24},{12,28},{16,0},{20,4},{24,8},{28,12},{1,17},{... | collective-permute-start | bytes 761864 | tf_op jit(solution)/shard_map/ppermute | solution.py:45
  412.9 40.3 %collective-permute-start.61 = (bf16[1,496,256]{2,1,0:T(8,128)(2,1)S(1)}, bf16[1,496,256]{2,1,0:T(8,128)(2,1)S(1)}, u32[]{:S(2)}, u32[]{:S(2)}) collective-permute-start(bf16[1,496,256]{2,1,0:T(8,128)(2,1)S(1)} %slice.510), channel_id=1, source_target_pairs={{0,16},{4,20},{8,24},{12,28},{16,0},{20,4},{24,8},{28,12},{1,17},{... | collective-permute-start | bytes 761864 | tf_op jit(solution)/shard_map/ppermute | solution.py:45
  415.9 38.4 %collective-permute-start.74 = (bf16[1,480,128]{2,1,0:T(8,128)(2,1)S(1)}, bf16[1,480,128]{2,1,0:T(8,128)(2,1)S(1)}, u32[]{:S(2)}, u32[]{:S(2)}) collective-permute-start(bf16[1,480,128]{2,1,0:T(8,128)(2,1)S(1)} %slice.536), channel_id=1, source_target_pairs={{0,8},{4,12},{8,0},{12,4},{16,24},{20,28},{24,16},{28,20},{1,9},{5... | collective-permute-start | bytes 368648 | tf_op jit(solution)/shard_map/ppermute | solution.py:45
  474.9 52.9 %collective-permute-start.51 = (bf16[1,128,1024]{2,1,0:T(8,128)(2,1)}, bf16[1,128,1024]{2,1,0:T(8,128)(2,1)}, u32[]{:S(2)}, u32[]{:S(2)}) collective-permute-start(bf16[1,128,1024]{2,1,0:T(8,128)(2,1)} %slice_bitcast_fusion.4), channel_id=1, source_target_pairs={{0,2},{1,3},{2,0},{3,1},{4,6},{5,7},{6,4},{7,5},{8,10},{9,11},{10,... | collective-permute-start | bytes 786440 | tf_op jit(solution)/shard_map/ppermute | solution.py:45
  475.7 54.6 %collective-permute-start.55 = (bf16[2,128,512]{2,1,0:T(8,128)(2,1)}, bf16[2,128,512]{2,1,0:T(8,128)(2,1)}, u32[]{:S(2)}, u32[]{:S(2)}) collective-permute-start(bf16[2,128,512]{2,1,0:T(8,128)(2,1)} %slice.498), channel_id=1, source_target_pairs={{0,4},{4,0},{8,12},{12,8},{16,20},{20,16},{24,28},{28,24},{1,5},{5... | collective-permute-start | bytes 786440 | tf_op jit(solution)/shard_map/ppermute | solution.py:45
  522.7 39.8 %collective-permute-start.43 = (bf16[1,384,1024]{2,1,0:T(8,128)(2,1)S(1)}, bf16[1,384,1024]{2,1,0:T(8,128)(2,1)}, u32[]{:S(2)}, u32[]{:S(2)}) collective-permute-start(bf16[1,384,1024]{2,1,0:T(8,128)(2,1)S(1)} %slice_bitcast_fusion.1), channel_id=1, source_target_pairs={{0,2},{1,3},{2,0},{3,1},{4,6},{5,7},{6,4},{7,5},{8,10},{9,11},{10,... | collective-permute-start | bytes 2359304 | tf_op jit(solution)/shard_map/ppermute | solution.py:45
  525.7 40.3 %collective-permute-start.47 = (bf16[2,384,512]{2,1,0:T(8,128)(2,1)}, bf16[2,384,512]{2,1,0:T(8,128)(2,1)}, u32[]{:S(2)}, u32[]{:S(2)}) collective-permute-start(bf16[2,384,512]{2,1,0:T(8,128)(2,1)} %slice.481), channel_id=1, source_target_pairs={{0,4},{4,0},{8,12},{12,8},{16,20},{20,16},{24,28},{28,24},{1,5},{5... | collective-permute-start | bytes 2359304 | tf_op jit(solution)/shard_map/ppermute | solution.py:45
  527.7 41.6 %collective-permute-start.42 = (bf16[512,1024]{1,0:T(8,128)(2,1)}, bf16[512,1024]{1,0:T(8,128)(2,1)}, u32[]{:S(2)}, u32[]{:S(2)}) collective-permute-start(bf16[512,1024]{1,0:T(8,128)(2,1)} %slice.617), channel_id=1, source_target_pairs={{0,1},{1,0},{2,3},{3,2},{4,5},{5,4},{6,7},{7,6},{8,9},{9,8},{10,11... | collective-permute-start | bytes 3145736 | tf_op jit(solution)/shard_map/ppermute | solution.py:45
  565.2 48.1 %collective-permute-start.44 = (bf16[1,384,512]{2,1,0:T(8,128)(2,1)}, bf16[1,384,512]{2,1,0:T(8,128)(2,1)}, u32[]{:S(2)}, u32[]{:S(2)}) collective-permute-start(bf16[1,384,512]{2,1,0:T(8,128)(2,1)} %slice.474), channel_id=1, source_target_pairs={{0,4},{4,0},{8,12},{12,8},{16,20},{20,16},{24,28},{28,24},{1,5},{5... | collective-permute-start | bytes 1179656 | tf_op jit(solution)/shard_map/ppermute | solution.py:45
  569.1 45.7 %collective-permute-start.48 = (bf16[1,384,512]{2,1,0:T(8,128)(2,1)}, bf16[1,384,512]{2,1,0:T(8,128)(2,1)}, u32[]{:S(2)}, u32[]{:S(2)}) collective-permute-start(bf16[1,384,512]{2,1,0:T(8,128)(2,1)} %slice.483), channel_id=1, source_target_pairs={{0,2},{1,3},{2,0},{3,1},{4,6},{5,7},{6,4},{7,5},{8,10},{9,11},{10,... | collective-permute-start | bytes 1179656 | tf_op jit(solution)/shard_map/ppermute | solution.py:45
  (133 other events, 1736.3 us)
